TPU v7x, 256 devices: a whole 4x4x8 slice. The times are simulated.
256 devices in a mesh: section: 64 (over x, y, z_hi, core), kv: 4 (over z_lo).
Axes of the slice: x: 4, y: 4, z: 8 (z_hi: 2, z_lo: 4; z = z_hi * 4 + z_lo), core: 2. Of those that a mesh axis runs over, the one named last changes fastest.
Arguments:
- query: bfloat16 [64, 512, 4096], P('section', None, 'kv'), parts along dimension 2, may hold values from -6 to 6
- grad_output: bfloat16 [64, 512, 4096], P('section', None, 'kv'), parts along dimension 2, may hold values from -150 to 150
- log_total: bfloat16 [64, 512, 32], P('section', None, 'kv'), parts along dimension 2, may hold values from -1 to 10, as said below
- offset: bfloat16 [64, 512, 32], P('section', None, 'kv'), parts along dimension 2, may hold values from -600 to 600
- slice_keys: bfloat16 [64, 512, 1024], P('section', None, 'kv'), parts along dimension 2, may hold values from -7 to 7
- pool_keys: bfloat16 [64, 1536, 1024], P('section', None, 'kv'), parts along dimension 2, may hold values from -7 to 7
- block_table: int32 [64, 3], P('section'), may hold values from 0 to 2, each once within a row
Outputs:
- query_grad: bfloat16 [64, 512, 4096], P('section', None, 'kv'), parts along dimension 2
- slice_grad: bfloat16 [64, 512, 1024], P('section', None, 'kv'), parts along dimension 2
- pool_grad: bfloat16 [64, 1536, 1024], P('section', None, 'kv'), parts along dimension 2
There are 4 independent parts, one for each index of `kv`. A program takes and returns all parts, laid end to end along the dimension named above; an argument that names none is the same for every part. Nothing has to cross between parts.
Inputs may be any that keep to these rules, and one draw needn't show every extreme that they name: Each row of block_table names every slot 0 to 2 once. log_total lies near the log of the count of visible keys of the row plus one half.
All inputs are finite; a program needn't handle non-finite values.
Results may differ from a plain program's by a relative error of at most 0.0051.
Values may be sent and summed in bfloat16 or wider, within the bound.
No kernel may reach another device: no remote copies, remote signals or barrier semaphores. Data moves between devices by JAX's collectives and lax.ppermute only.
A program may use at most 128 MiB of HBM per device.

v0:
```python
import jax
import jax.numpy as jnp
from jax import lax
from jax.sharding import PartitionSpec as P

NSL = 4


def passed_along(x, axis, by):
    length = lax.axis_size(axis)
    return lax.ppermute(x, axis, [(i, (i + by) % length) for i in range(length)])


def block_terms(queries, out_grads, totals, offsets, key_data, value_data, causal):
    score_scale = key_data.shape[1] ** (-0.5)
    scores = (
        jnp.einsum("rhd,cd->rhc", queries, key_data, preferred_element_type=jnp.float32)
        * score_scale
    )
    weights = jnp.exp(scores - totals.astype(jnp.float32)[:, :, None])
    if causal:
        row_ids = jnp.arange(queries.shape[0], dtype=jnp.int32)
        visible = row_ids[:, None] >= row_ids[None, :]
        weights = jnp.where(visible[:, None, :], weights, jnp.zeros_like(weights))
    weight_grad = jnp.einsum(
        "rhd,cd->rhc", out_grads, value_data, preferred_element_type=jnp.float32
    )
    score_grad = weights * (weight_grad - offsets.astype(jnp.float32)[:, :, None])
    weights_low = weights.astype(jnp.bfloat16)
    score_low = score_grad.astype(jnp.bfloat16)
    query_part = (
        jnp.einsum("rhc,cd->rhd", score_low, key_data, preferred_element_type=jnp.float32)
        * score_scale
    )
    key_part = (
        jnp.einsum("rhc,rhd->cd", score_low, queries, preferred_element_type=jnp.float32)
        * score_scale
    )
    value_part = jnp.einsum(
        "rhc,rhd->cd", weights_low, out_grads, preferred_element_type=jnp.float32
    )
    return (query_part, jnp.concatenate([key_part, value_part], axis=1))


def pool_terms(queries, out_grads, totals, offsets, pool_block, slot_order, block_count):
    head_size = pool_block.shape[1] // 2
    slice_rows = queries.shape[0]
    query_sum = jnp.zeros(queries.shape, jnp.float32)
    pool_sum = jnp.zeros(pool_block.shape, jnp.float32)

    def add_block(position, carry):
        query_acc, grad_acc = carry
        row_start = slot_order[position] * slice_rows
        key_block = lax.dynamic_slice_in_dim(pool_block, row_start, slice_rows, 0)
        query_part, block_grad = block_terms(
            queries,
            out_grads,
            totals,
            offsets,
            key_block[:, :head_size],
            key_block[:, head_size:],
            False,
        )
        grad_acc = lax.dynamic_update_slice_in_dim(grad_acc, block_grad, row_start, 0)
        return (query_acc + query_part, grad_acc)

    return lax.fori_loop(0, block_count, add_block, (query_sum, pool_sum))


def per_device(query, grad_output, log_total, offset, slice_keys, pool_keys, block_table):
    slice_rows = slice_keys.shape[1]
    head_size = slice_keys.shape[2] // 2
    head_count = log_total.shape[2]
    queries = query[0].reshape(slice_rows, head_count, head_size)
    out_grads = grad_output[0].reshape(slice_rows, head_count, head_size)
    totals = log_total[0]
    offsets = offset[0]
    own_block = slice_keys[0]
    pool_block = pool_keys[0]
    slot_order = block_table[0]
    sections = lax.axis_size("section")
    half_axis = sections // 2
    group_size = sections // NSL
    layer_index = lax.axis_index("section")
    own_query, own_grad = block_terms(
        queries,
        out_grads,
        totals,
        offsets,
        own_block[:, :head_size],
        own_block[:, head_size:],
        True,
    )
    arrived = passed_along((query[0], grad_output[0], totals, offsets), "section", half_axis)
    partner_index = (layer_index - half_axis) % sections
    partner_depth = NSL - 1 - partner_index // group_size % (NSL - 1)
    lent_queries = arrived[0].reshape(slice_rows, head_count, head_size)
    lent_grads = arrived[1].reshape(slice_rows, head_count, head_size)
    lent_query, pool_sum = pool_terms(
        lent_queries, lent_grads, arrived[2], arrived[3], pool_block, slot_order, partner_depth
    )
    returned = passed_along(
        lent_query.reshape(slice_rows, head_count * head_size).astype(jnp.bfloat16),
        "section",
        -half_axis,
    )
    query_sum = own_query + returned.astype(jnp.float32).reshape(slice_rows, head_count, head_size)
    query_grad = query_sum.reshape(slice_rows, head_count * head_size).astype(jnp.bfloat16)[None]
    return (query_grad, own_grad.astype(jnp.bfloat16)[None], pool_sum.astype(jnp.bfloat16)[None])


def solution(mesh):
    return jax.shard_map(
        per_device,
        mesh=mesh,
        in_specs=(
            P("section", None, "kv"),
            P("section", None, "kv"),
            P("section", None, "kv"),
            P("section", None, "kv"),
            P("section", None, "kv"),
            P("section", None, "kv"),
            P("section", None),
        ),
        out_specs=(P("section", None, "kv"), P("section", None, "kv"), P("section", None, "kv")),
        check_vma=False,
    )
```

profile of v0, /device:TPU:28, one launch (start us, length us, event | category | flops | bytes accessed | tf_op | source)
XLA Modules:
  0.0 146.4 jit_solution(11037057173317763180)
XLA Ops:
  0.6 0.0 copy-start.6
  0.6 0.6 collective-permute-start
  1.2 3.0 %collective-permute-start.2 = (bf16[512,1024]{1,0:T(8,128)(2,1)}, bf16[512,1024]{1,0:T(8,128)(2,1)S(1)}, u32[]{:S(2)}, u32[]{:S(2)}) collective-permute-start(bf16[512,1024]{1,0:T(8,128)(2,1)} %bitcast.115), channel_id=1, source_target_pairs={{0,128},{4,132},{8,136},{12,140},{16,144},{20,148},{24,152},{28,15... | collective-permute-start | bytes 3145736 | tf_op jit(solution)/shard_map/ppermute | solution.py:11
  4.3 0.5 collective-permute-start.1
  4.8 3.0 %collective-permute-start.3 = (bf16[512,8]{0,1:T(8,128)(2,1)}, bf16[512,8]{0,1:T(8,128)(2,1)S(1)}, u32[]{:S(2)}, u32[]{:S(2)}) collective-permute-start(bf16[512,8]{0,1:T(8,128)(2,1)} %bitcast.124), channel_id=1, source_target_pairs={{0,128},{4,132},{8,136},{12,140},{16,144},{20,148},{24,152},{28,15... | collective-permute-start | bytes 24584 | tf_op jit(solution)/shard_map/ppermute | solution.py:11
  7.8 1.5 %copy.50 = bf16[1,512,1024]{1,2,0:T(8,128)(2,1)S(1)} copy(bf16[1,512,1024]{2,1,0:T(8,128)(2,1)} %param.9) | data formatting | bytes 2097152 | tf_op jit(solution)/shard_map/reshape;squeeze | solution.py:74
  9.3 1.5 %copy.51 = bf16[1,512,1024]{1,2,0:T(8,128)(2,1)S(1)} copy(bf16[1,512,1024]{2,1,0:T(8,128)(2,1)} %param.10) | data formatting | bytes 2097152 | tf_op jit(solution)/shard_map/reshape;squeeze | solution.py:75
  10.8 0.1 iota_compare_fusion
  10.9 0.0 copy-start.8
  10.9 0.7 bitcast_convert_fusion.1
  11.7 0.7 bitcast_convert_fusion
  12.4 2.2 %fusion.31 = f32[512,8,512]{2,0,1:T(8,128)S(1)} fusion(bf16[512,8,128]{0,2,1:T(8,128)(2,1)S(1)} %bitcast.109, bf16[512,256]{1,0:T(8,128)(2,1)} %bitcast.120), kind=kOutput, calls=%fused_computation.38 | convolution fusion | flops 536870912 | bytes 9568256 | tf_op jit(solution)/shard_map/rhd,cd->rhc/dot_general | solution.py:17
  14.6 3.5 %multiply_convert_fusion.1 = bf16[512,8,512]{2,0,1:T(8,128)(2,1)S(1)} fusion(f32[512,8,512]{2,0,1:T(8,128)S(1)} %fusion.31, f32[512,8]{0,1:T(8,128)S(1)} %bitcast_convert_fusion, f32[512,8]{0,1:T(8,128)S(1)} %bitcast_convert_fusion.1, pred[512,512]{1,0:T(8,128)(4,1)S(1)} %iota_compare_fusion, bf16[512,8,128]{0,2,1:T(8,128)(2,1)S(1)} %bitcast.116, ...), kind=kOutput, calls=%fused_computation.18 | convolution fusion | flops 549453824 | bytes 14057472 | tf_op jit(solution)/shard_map/rhd,cd->rhc/dot_general | solution.py:25
  18.1 1.9 %copy-done.3 = bf16[512,8,512]{2,0,1:T(8,128)(2,1)} copy-done((bf16[512,8,512]{2,0,1:T(8,128)(2,1)}, bf16[512,8,512]{2,0,1:T(8,128)(2,1)S(1)}, u32[]{:S(2)}) %copy-start.3) | copy-done | bytes 4194328
  20.1 0.7 fusion.26
  20.8 0.0 copy-done.4
  20.8 7.7 %collective-permute-done = bf16[512,1024]{1,0:T(8,128)(2,1)} collective-permute-done((bf16[512,1024]{1,0:T(8,128)(2,1)}, bf16[512,1024]{1,0:T(8,128)(2,1)}, u32[]{:S(2)}, u32[]{:S(2)}) %collective-permute-start) | collective-permute-done | bytes 1048608 | tf_op jit(solution)/shard_map/ppermute | solution.py:11
  28.6 1.5 %copy.33 = bf16[512,1024]{0,1:T(8,128)(2,1)S(1)} copy(bf16[512,1024]{1,0:T(8,128)(2,1)} %collective-permute-done) | data formatting | bytes 2097152 | tf_op jit(solution)/shard_map/ppermute | solution.py:11
  30.1 19.9 %collective-permute-done.2 = bf16[512,1024]{1,0:T(8,128)(2,1)S(1)} collective-permute-done((bf16[512,1024]{1,0:T(8,128)(2,1)}, bf16[512,1024]{1,0:T(8,128)(2,1)S(1)}, u32[]{:S(2)}, u32[]{:S(2)}) %collective-permute-start.2) | collective-permute-done | bytes 1048608 | tf_op jit(solution)/shard_map/ppermute | solution.py:11
  50.0 1.3 copy.34
  51.3 0.0 collective-permute-done.1
  51.3 0.0 collective-permute-done.3
  51.3 0.1 broadcast_in_dim.20
  51.5 0.9 broadcast_in_dim.32.clone
  52.4 0.0 copy-done.10
  52.4 66.2 %while.12 = (s32[]{:T(128)}, f32[512,8,128]{2,0,1:T(8,128)S(1)}, bf16[1536,256]{1,0:T(8,128)(2,1)}, s32[]{:T(128)}, s32[3]{0:T(128)S(1)}, /*index=5*/bf16[1536,2...) while((s32[]{:T(128)}, f32[512,8,128]{2,0,1:T(8,128)S(1)}, ...), condition=%wide.region_1.2_spmd, body=%wide.region_0.1_spmd.sunk | while | flops 2702843904 | bytes 102990272 | solution.py:67
  52.4 0.6 dynamic_slice.7
  53.6 5.4 %fusion.64 = f32[512,512,8]{1,0,2:T(8,128)} fusion(bf16[512,8,128]{0,2,1:T(8,128)(2,1)S(1)} %get-tuple-element.185, bf16[1536,256]{1,0:T(8,128)(2,1)} %get-tuple-element.184, s32[]{:T(128)S(6)} %select_n.45), kind=kOutput, calls=%fused_computation.13.clone.1 | convolution fusion | flops 536870912 | bytes 9568260 | tf_op jit(solution)/shard_map/while/body/rhd,cd->rhc/dot_general | solution.py:17
  59.0 0.0 copy-start.2
  59.0 5.9 %fusion.65 = bf16[512,8,512]{0,2,1:T(8,128)(2,1)S(1)} fusion(f32[512,512,8]{1,0,2:T(8,128)} %fusion.64, f32[512,8]{0,1:T(8,128)S(1)} %convert_element_type.104, f32[512,8]{0,1:T(8,128)S(1)} %convert_element_type.105, bf16[512,8,128]{0,2,1:T(8,128)(2,1)} %get-tuple-element.187, bf16[1536,256]{1,0:T(8,128)(2,1)} %get-tuple-element.184, ...), kind=kOutput, calls=%fused_computation.4.clone.1 | convolution fusion | flops 547356672 | bytes 13795336 | tf_op jit(solution)/shard_map/while/body/rhd,cd->rhc/dot_general | solution.py:25
  64.9 0.0 copy-start.1
  64.9 1.4 fusion.67
  66.4 1.7 %fusion.66 = bf16[512,128]{0,1:T(8,128)(2,1)S(1)} fusion(bf16[512,8,128]{0,2,1:T(8,128)(2,1)S(1)} %copy-done.2, f32[512,512,8]{1,0,2:T(8,128)S(1)} %copy-done, f32[512,8]{0,1:T(8,128)S(1)} %convert_element_type.105), kind=kOutput, calls=%fused_computation.9.clone.1 | convolution fusion | flops 543162368 | bytes 9584640 | tf_op jit(solution)/shard_map/while/body/rhc,rhd->cd/dot_general | solution.py:39
  68.1 0.8 copy.53
  69.0 1.7 %constant_dynamic-update-slice_fusion.2 = bf16[1536,256]{1,0:T(8,128)(2,1)} fusion(bf16[1536,256]{1,0:T(8,128)(2,1)} %get-tuple-element.165, bf16[512,256]{1,0:T(8,128)(2,1)} %copy.53, s32[]{:T(128)S(6)} %select_n.45), kind=kLoop, calls=%fused_computation.16.clone.1 | loop fusion | bytes 524292 | tf_op jit(solution)/shard_map/while/body/dynamic_update_slice | solution.py:64
  70.7 3.8 %multiply_add_fusion.2 = f32[512,8,128]{2,0,1:T(8,128)S(1)} fusion(f32[512,8,128]{2,0,1:T(8,128)S(1)} %get-tuple-element.164, bf16[512,8,512]{0,2,1:T(8,128)(2,1)} %copy-done.1, bf16[1536,256]{1,0:T(8,128)(2,1)} %get-tuple-element.184, s32[]{:T(128)S(6)} %select_n.45), kind=kOutput, calls=%fused_computation.6.clone.1 | convolution fusion | flops 537919488 | bytes 8519684 | tf_op jit(solution)/shard_map/while/body/rhc,cd->rhd/dot_general | solution.py:32
  74.5 0.6 dynamic_slice.7
  75.7 5.4 %fusion.64 = f32[512,512,8]{1,0,2:T(8,128)} fusion(bf16[512,8,128]{0,2,1:T(8,128)(2,1)S(1)} %get-tuple-element.185, bf16[1536,256]{1,0:T(8,128)(2,1)} %get-tuple-element.184, s32[]{:T(128)S(6)} %select_n.45), kind=kOutput, calls=%fused_computation.13.clone.1 | convolution fusion | flops 536870912 | bytes 9568260 | tf_op jit(solution)/shard_map/while/body/rhd,cd->rhc/dot_general | solution.py:17
  81.1 0.0 copy-start.2
  81.1 5.9 %fusion.65 = bf16[512,8,512]{0,2,1:T(8,128)(2,1)S(1)} fusion(f32[512,512,8]{1,0,2:T(8,128)} %fusion.64, f32[512,8]{0,1:T(8,128)S(1)} %convert_element_type.104, f32[512,8]{0,1:T(8,128)S(1)} %convert_element_type.105, bf16[512,8,128]{0,2,1:T(8,128)(2,1)} %get-tuple-element.187, bf16[1536,256]{1,0:T(8,128)(2,1)} %get-tuple-element.184, ...), kind=kOutput, calls=%fused_computation.4.clone.1 | convolution fusion | flops 547356672 | bytes 13795336 | tf_op jit(solution)/shard_map/while/body/rhd,cd->rhc/dot_general | solution.py:25
  87.0 0.0 copy-start.1
  87.0 1.4 fusion.67
  88.5 1.7 %fusion.66 = bf16[512,128]{0,1:T(8,128)(2,1)S(1)} fusion(bf16[512,8,128]{0,2,1:T(8,128)(2,1)S(1)} %copy-done.2, f32[512,512,8]{1,0,2:T(8,128)S(1)} %copy-done, f32[512,8]{0,1:T(8,128)S(1)} %convert_element_type.105), kind=kOutput, calls=%fused_computation.9.clone.1 | convolution fusion | flops 543162368 | bytes 9584640 | tf_op jit(solution)/shard_map/while/body/rhc,rhd->cd/dot_general | solution.py:39
  90.2 0.8 copy.53
  91.1 1.7 %constant_dynamic-update-slice_fusion.2 = bf16[1536,256]{1,0:T(8,128)(2,1)} fusion(bf16[1536,256]{1,0:T(8,128)(2,1)} %get-tuple-element.165, bf16[512,256]{1,0:T(8,128)(2,1)} %copy.53, s32[]{:T(128)S(6)} %select_n.45), kind=kLoop, calls=%fused_computation.16.clone.1 | loop fusion | bytes 524292 | tf_op jit(solution)/shard_map/while/body/dynamic_update_slice | solution.py:64
  92.7 3.8 %multiply_add_fusion.2 = f32[512,8,128]{2,0,1:T(8,128)S(1)} fusion(f32[512,8,128]{2,0,1:T(8,128)S(1)} %get-tuple-element.164, bf16[512,8,512]{0,2,1:T(8,128)(2,1)} %copy-done.1, bf16[1536,256]{1,0:T(8,128)(2,1)} %get-tuple-element.184, s32[]{:T(128)S(6)} %select_n.45), kind=kOutput, calls=%fused_computation.6.clone.1 | convolution fusion | flops 537919488 | bytes 8519684 | tf_op jit(solution)/shard_map/while/body/rhc,cd->rhd/dot_general | solution.py:32
  96.5 0.6 dynamic_slice.7
  97.8 5.4 %fusion.64 = f32[512,512,8]{1,0,2:T(8,128)} fusion(bf16[512,8,128]{0,2,1:T(8,128)(2,1)S(1)} %get-tuple-element.185, bf16[1536,256]{1,0:T(8,128)(2,1)} %get-tuple-element.184, s32[]{:T(128)S(6)} %select_n.45), kind=kOutput, calls=%fused_computation.13.clone.1 | convolution fusion | flops 536870912 | bytes 9568260 | tf_op jit(solution)/shard_map/while/body/rhd,cd->rhc/dot_general | solution.py:17
  103.2 0.0 copy-start.2
  103.2 5.9 %fusion.65 = bf16[512,8,512]{0,2,1:T(8,128)(2,1)S(1)} fusion(f32[512,512,8]{1,0,2:T(8,128)} %fusion.64, f32[512,8]{0,1:T(8,128)S(1)} %convert_element_type.104, f32[512,8]{0,1:T(8,128)S(1)} %convert_element_type.105, bf16[512,8,128]{0,2,1:T(8,128)(2,1)} %get-tuple-element.187, bf16[1536,256]{1,0:T(8,128)(2,1)} %get-tuple-element.184, ...), kind=kOutput, calls=%fused_computation.4.clone.1 | convolution fusion | flops 547356672 | bytes 13795336 | tf_op jit(solution)/shard_map/while/body/rhd,cd->rhc/dot_general | solution.py:25
  109.1 1.4 fusion.67
  110.6 1.7 %fusion.66 = bf16[512,128]{0,1:T(8,128)(2,1)S(1)} fusion(bf16[512,8,128]{0,2,1:T(8,128)(2,1)S(1)} %copy-done.2, f32[512,512,8]{1,0,2:T(8,128)S(1)} %copy-done, f32[512,8]{0,1:T(8,128)S(1)} %convert_element_type.105), kind=kOutput, calls=%fused_computation.9.clone.1 | convolution fusion | flops 543162368 | bytes 9584640 | tf_op jit(solution)/shard_map/while/body/rhc,rhd->cd/dot_general | solution.py:39
  112.3 0.8 copy.53
  113.1 1.7 %constant_dynamic-update-slice_fusion.2 = bf16[1536,256]{1,0:T(8,128)(2,1)} fusion(bf16[1536,256]{1,0:T(8,128)(2,1)} %get-tuple-element.165, bf16[512,256]{1,0:T(8,128)(2,1)} %copy.53, s32[]{:T(128)S(6)} %select_n.45), kind=kLoop, calls=%fused_computation.16.clone.1 | loop fusion | bytes 524292 | tf_op jit(solution)/shard_map/while/body/dynamic_update_slice | solution.py:64
  114.8 3.8 %multiply_add_fusion.2 = f32[512,8,128]{2,0,1:T(8,128)S(1)} fusion(f32[512,8,128]{2,0,1:T(8,128)S(1)} %get-tuple-element.164, bf16[512,8,512]{0,2,1:T(8,128)(2,1)} %copy-done.1, bf16[1536,256]{1,0:T(8,128)(2,1)} %get-tuple-element.184, s32[]{:T(128)S(6)} %select_n.45), kind=kOutput, calls=%fused_computation.6.clone.1 | convolution fusion | flops 537919488 | bytes 8519684 | tf_op jit(solution)/shard_map/while/body/rhc,cd->rhd/dot_general | solution.py:32
  118.6 0.0 copy-start.7
  118.6 0.6 copy.35
  119.2 0.1 collective-permute-start.4
  119.3 5.6 %fusion.27 = bf16[1,512,128]{1,2,0:T(8,128)(2,1)S(1)} fusion(bf16[512,8,128]{0,2,1:T(8,128)(2,1)} %bitcast.117, f32[512,8,512]{2,0,1:T(8,128)} %copy-done.4, f32[512,8]{0,1:T(8,128)} %copy-done.9, pred[512,512]{1,0:T(8,128)(4,1)} %copy-done.8), kind=kOutput, calls=%fused_computation.31 | convolution fusion | flops 545325056 | bytes 9846784 | tf_op jit(solution)/shard_map/rhc,rhd->cd/dot_general | solution.py:39
  124.9 0.8 copy.40
  125.8 3.7 %fusion.30 = f32[512,8,128]{0,2,1:T(8,128)S(1)} fusion(bf16[512,8,512]{2,0,1:T(8,128)(2,1)} %copy-done.3, bf16[512,256]{1,0:T(8,128)(2,1)S(1)} %bitcast.122), kind=kOutput, calls=%fused_computation.37 | convolution fusion | flops 536870912 | bytes 6422528 | tf_op jit(solution)/shard_map/rhc,cd->rhd/dot_general | solution.py:32
  129.5 15.2 %collective-permute-done.4 = bf16[512,1024]{0,1:T(8,128)(2,1)S(1)} collective-permute-done((bf16[512,1024]{0,1:T(8,128)(2,1)S(1)}, bf16[512,1024]{0,1:T(8,128)(2,1)S(1)}, u32[]{:S(2)}, u32[]{:S(2)}) %collective-permute-start.4) | collective-permute-done | bytes 1048608 | tf_op jit(solution)/shard_map/ppermute | solution.py:11
  144.7 0.4 fusion.17
  145.1 1.3 copy.39
  (39 shorter events, 0.2 us)
Async XLA Ops:
  0.6 13.9 %copy-start.6 = (bf16[1,512,256]{2,1,0:T(8,128)(2,1)S(1)}, bf16[1,512,256]{2,1,0:T(8,128)(2,1)}, u32[]{:S(2)}) copy-start(bf16[1,512,256]{2,1,0:T(8,128)(2,1)} %param.13) | copy-start | bytes 786436
  0.6 27.9 %collective-permute-start = (bf16[512,1024]{1,0:T(8,128)(2,1)}, bf16[512,1024]{1,0:T(8,128)(2,1)}, u32[]{:S(2)}, u32[]{:S(2)}) collective-permute-start(bf16[512,1024]{1,0:T(8,128)(2,1)} %bitcast.114), channel_id=1, source_target_pairs={{0,128},{4,132},{8,136},{12,140},{16,144},{20,148},{24,152},{28,15... | collective-permute-start | bytes 3145736 | tf_op jit(solution)/shard_map/ppermute | solution.py:11
  1.2 48.8 %collective-permute-start.2 = (bf16[512,1024]{1,0:T(8,128)(2,1)}, bf16[512,1024]{1,0:T(8,128)(2,1)S(1)}, u32[]{:S(2)}, u32[]{:S(2)}) collective-permute-start(bf16[512,1024]{1,0:T(8,128)(2,1)} %bitcast.115), channel_id=1, source_target_pairs={{0,128},{4,132},{8,136},{12,140},{16,144},{20,148},{24,152},{28,15... | collective-permute-start | bytes 3145736 | tf_op jit(solution)/shard_map/ppermute | solution.py:11
  4.3 47.0 %collective-permute-start.1 = (bf16[512,8]{0,1:T(8,128)(2,1)}, bf16[512,8]{0,1:T(8,128)(2,1)S(1)}, u32[]{:S(2)}, u32[]{:S(2)}) collective-permute-start(bf16[512,8]{0,1:T(8,128)(2,1)} %bitcast.123), channel_id=1, source_target_pairs={{0,128},{4,132},{8,136},{12,140},{16,144},{20,148},{24,152},{28,15... | collective-permute-start | bytes 24584 | tf_op jit(solution)/shard_map/ppermute | solution.py:11
  4.8 46.5 %collective-permute-start.3 = (bf16[512,8]{0,1:T(8,128)(2,1)}, bf16[512,8]{0,1:T(8,128)(2,1)S(1)}, u32[]{:S(2)}, u32[]{:S(2)}) collective-permute-start(bf16[512,8]{0,1:T(8,128)(2,1)} %bitcast.124), channel_id=1, source_target_pairs={{0,128},{4,132},{8,136},{12,140},{16,144},{20,148},{24,152},{28,15... | collective-permute-start | bytes 24584 | tf_op jit(solution)/shard_map/ppermute | solution.py:11
  10.8 7.3 %copy-start.5 = (bf16[1,512,1024]{1,2,0:T(8,128)(2,1)}, bf16[1,512,1024]{1,2,0:T(8,128)(2,1)S(1)}, u32[]{:S(2)}) copy-start(bf16[1,512,1024]{1,2,0:T(8,128)(2,1)S(1)} %copy.51) | copy-start | bytes 3145732
  10.9 7.2 %copy-start.8 = (pred[512,512]{1,0:T(8,128)(4,1)}, pred[512,512]{1,0:T(8,128)(4,1)S(1)}, u32[]{:S(2)}) copy-start(pred[512,512]{1,0:T(8,128)(4,1)S(1)} %iota_compare_fusion) | copy-start | bytes 786436
  11.7 2.9 %copy-start.9 = (f32[512,8]{0,1:T(8,128)}, f32[512,8]{0,1:T(8,128)S(1)}, u32[]{:S(2)}) copy-start(f32[512,8]{0,1:T(8,128)S(1)} %bitcast_convert_fusion.1) | copy-start | bytes 49156
  14.5 6.2 %copy-start.4 = (f32[512,8,512]{2,0,1:T(8,128)}, f32[512,8,512]{2,0,1:T(8,128)S(1)}, u32[]{:S(2)}) copy-start(f32[512,8,512]{2,0,1:T(8,128)S(1)} %fusion.31) | copy-start | bytes 25165828
  18.1 2.0 %copy-start.3 = (bf16[512,8,512]{2,0,1:T(8,128)(2,1)}, bf16[512,8,512]{2,0,1:T(8,128)(2,1)S(1)}, u32[]{:S(2)}) copy-start(bf16[512,8,512]{2,0,1:T(8,128)(2,1)S(1)} %multiply_convert_fusion.1) | copy-start | bytes 12582916
  20.1 32.3 %copy-start.10 = (s32[1,3]{1,0:T(1,128)S(1)}, s32[1,3]{1,0:T(1,128)}, u32[]{:S(2)}) copy-start(s32[1,3]{1,0:T(1,128)} %param.15) | copy-start | bytes 40
  59.0 7.4 %copy-start = (f32[512,512,8]{1,0,2:T(8,128)S(1)}, f32[512,512,8]{1,0,2:T(8,128)}, u32[]{:S(2)}) copy-start(f32[512,512,8]{1,0,2:T(8,128)} %fusion.64) | copy-start | bytes 25165828 | tf_op jit(solution)/shard_map/while
  59.0 7.4 %copy-start.2 = (bf16[512,8,128]{0,2,1:T(8,128)(2,1)S(1)}, bf16[512,8,128]{0,2,1:T(8,128)(2,1)}, u32[]{:S(2)}) copy-start(bf16[512,8,128]{0,2,1:T(8,128)(2,1)} %get-tuple-element.187) | copy-start | bytes 3145732 | tf_op jit(solution)/shard_map/while
  64.9 3.2 %copy-start.1 = (bf16[512,8,512]{0,2,1:T(8,128)(2,1)}, bf16[512,8,512]{0,2,1:T(8,128)(2,1)S(1)}, u32[]{:S(2)}) copy-start(bf16[512,8,512]{0,2,1:T(8,128)(2,1)S(1)} %fusion.65) | copy-start | bytes 12582916 | tf_op jit(solution)/shard_map/while
  69.0 5.5 %copy-start.11 = (s32[1,3]{1,0:T(1,128)S(1)}, s32[1,3]{1,0:T(1,128)}, u32[]{:S(2)}) copy-start(s32[1,3]{1,0:T(1,128)} %get-tuple-element.220) | copy-start | bytes 40 | tf_op jit(solution)/shard_map/while
  81.1 7.4 %copy-start = (f32[512,512,8]{1,0,2:T(8,128)S(1)}, f32[512,512,8]{1,0,2:T(8,128)}, u32[]{:S(2)}) copy-start(f32[512,512,8]{1,0,2:T(8,128)} %fusion.64) | copy-start | bytes 25165828 | tf_op jit(solution)/shard_map/while
  81.1 7.4 %copy-start.2 = (bf16[512,8,128]{0,2,1:T(8,128)(2,1)S(1)}, bf16[512,8,128]{0,2,1:T(8,128)(2,1)}, u32[]{:S(2)}) copy-start(bf16[512,8,128]{0,2,1:T(8,128)(2,1)} %get-tuple-element.187) | copy-start | bytes 3145732 | tf_op jit(solution)/shard_map/while
  87.0 3.2 %copy-start.1 = (bf16[512,8,512]{0,2,1:T(8,128)(2,1)}, bf16[512,8,512]{0,2,1:T(8,128)(2,1)S(1)}, u32[]{:S(2)}) copy-start(bf16[512,8,512]{0,2,1:T(8,128)(2,1)S(1)} %fusion.65) | copy-start | bytes 12582916 | tf_op jit(solution)/shard_map/while
  91.1 5.5 %copy-start.11 = (s32[1,3]{1,0:T(1,128)S(1)}, s32[1,3]{1,0:T(1,128)}, u32[]{:S(2)}) copy-start(s32[1,3]{1,0:T(1,128)} %get-tuple-element.220) | copy-start | bytes 40 | tf_op jit(solution)/shard_map/while
  103.2 7.4 %copy-start = (f32[512,512,8]{1,0,2:T(8,128)S(1)}, f32[512,512,8]{1,0,2:T(8,128)}, u32[]{:S(2)}) copy-start(f32[512,512,8]{1,0,2:T(8,128)} %fusion.64) | copy-start | bytes 25165828 | tf_op jit(solution)/shard_map/while
  103.2 7.4 %copy-start.2 = (bf16[512,8,128]{0,2,1:T(8,128)(2,1)S(1)}, bf16[512,8,128]{0,2,1:T(8,128)(2,1)}, u32[]{:S(2)}) copy-start(bf16[512,8,128]{0,2,1:T(8,128)(2,1)} %get-tuple-element.187) | copy-start | bytes 3145732 | tf_op jit(solution)/shard_map/while
  109.1 3.2 %copy-start.1 = (bf16[512,8,512]{0,2,1:T(8,128)(2,1)}, bf16[512,8,512]{0,2,1:T(8,128)(2,1)S(1)}, u32[]{:S(2)}) copy-start(bf16[512,8,512]{0,2,1:T(8,128)(2,1)S(1)} %fusion.65) | copy-start | bytes 12582916 | tf_op jit(solution)/shard_map/while
  113.1 5.5 %copy-start.11 = (s32[1,3]{1,0:T(1,128)S(1)}, s32[1,3]{1,0:T(1,128)}, u32[]{:S(2)}) copy-start(s32[1,3]{1,0:T(1,128)} %get-tuple-element.220) | copy-start | bytes 40 | tf_op jit(solution)/shard_map/while
  118.6 7.2 %copy-start.7 = (bf16[1,512,256]{2,1,0:T(8,128)(2,1)S(1)}, bf16[1,512,256]{2,1,0:T(8,128)(2,1)}, u32[]{:S(2)}) copy-start(bf16[1,512,256]{2,1,0:T(8,128)(2,1)} %param.13) | copy-start | bytes 786436
  119.2 25.5 %collective-permute-start.4 = (bf16[512,1024]{0,1:T(8,128)(2,1)S(1)}, bf16[512,1024]{0,1:T(8,128)(2,1)S(1)}, u32[]{:S(2)}, u32[]{:S(2)}) collective-permute-start(bf16[512,1024]{0,1:T(8,128)(2,1)S(1)} %bitcast.113), channel_id=1, source_target_pairs={{0,128},{4,132},{8,136},{12,140},{16,144},{20,148},{24,152},{28,15... | collective-permute-start | bytes 3145736 | tf_op jit(solution)/shard_map/ppermute | solution.py:11
where the time goes:
time: 147 us; the launch traced here: 146 us
  matrix products  70.1 us (48%)
  waiting for transfers between devices  42.9 us (29%)
  local copies, waits for them, and re-layouts  21 us (14%)
  starting transfers between devices  7.24 us (5%)
  loops' own time  2.23 us (2%)
  other arithmetic  2.06 us (1%)
    ppermute x5, waiting for transfers between devices, passed_along(): lax.ppermute(x, axis, [(i, (i + by) % length) for i in range(length)])  42.9 us
    dot_general x4, matrix products, block_terms(): jnp.einsum('rhd,cd->rhc', out_grads, value_data, preferred_element_type=j...  21.2 us
    dot_general x4, matrix products, block_terms(): jnp.einsum('rhd,cd->rhc', queries, key_data, preferred_element_type=jnp.f...  18.4 us
    dot_general x4, matrix products, block_terms(): jnp.einsum('rhc,cd->rhd', score_low, key_data, preferred_element_type=jnp...  15 us
    dot_general x4, matrix products, block_terms(): jnp.einsum('rhc,rhd->cd', weights_low, out_grads, preferred_element_type=...  10.6 us
    dynamic_update_slice x6, local copies, waits for them, and re-layouts, add_block(): lax.dynamic_update_slice_in_dim(grad_acc, block_grad, row_start, 0)  7.55 us
    ppermute x5, starting transfers between devices, passed_along(): lax.ppermute(x, axis, [(i, (i + by) % length) for i in range(length)])  7.24 us
    dot_general x4, matrix products, block_terms(): jnp.einsum('rhc,rhd->cd', score_low, queries, preferred_element_type=jnp....  5.06 us
  transfers between devices with their start and end apart: 5, of which 3 were waited for; matrix products, arithmetic and copies ran while one was open for 16% of the time, Pallas kernels for 0%

commit v1 on v0

v1 whole, which is shorter than its diff:
```python
import functools

import jax
import jax.numpy as jnp
from jax import lax
from jax.experimental import pallas as pl
from jax.experimental.pallas import tpu as pltpu
from jax.sharding import PartitionSpec as P


NSL = 4
LOG2E = 1.4426950408889634
F32 = jnp.float32
BF16 = jnp.bfloat16
VMEM = pl.BlockSpec(memory_space=pltpu.VMEM)
SMEM = pl.BlockSpec(memory_space=pltpu.SMEM)
HBM = pl.BlockSpec(memory_space=pltpu.HBM)
PIECES = ((0, 0, 512), (1, 0, 512), (2, 0, 512))


def dot(a, b, ca, cb):
    return lax.dot_general(a, b, (((ca,), (cb,)), ((), ())), preferred_element_type=F32)


def in_hbm(x):
    return pltpu.with_memory_space_constraint(x, pltpu.HBM)


def params(mib):
    return pltpu.CompilerParams(vmem_limit_bytes=mib << 20)


def cost(rows, keys, heads, dh):
    return pl.CostEstimate(
        flops=10 * rows * keys * heads * dh, bytes_accessed=1 << 20, transcendentals=rows * keys * heads
    )


def pick_kernel(rows, table_ref, pool_ref, *refs):
    outs, sem = refs[:-1], refs[-1]
    copies = []
    for i, (block, first, size) in enumerate(PIECES):
        at = pl.multiple_of(table_ref[block] * rows + first, 128)
        copies.append(pltpu.make_async_copy(pool_ref.at[pl.ds(at, size), :], outs[i], sem.at[i]))
    for c in copies:
        c.start()
    for c in copies:
        c.wait()


def pick(table, pool, rows):
    width = pool.shape[1]
    return pl.pallas_call(
        functools.partial(pick_kernel, rows),
        in_specs=[SMEM, HBM],
        out_specs=[VMEM] * len(PIECES),
        out_shape=[jax.ShapeDtypeStruct((size, width), pool.dtype) for _, _, size in PIECES],
        scratch_shapes=[pltpu.SemaphoreType.DMA((len(PIECES),))],
        compiler_params=params(4),
        name="pick",
    )(table, in_hbm(pool))


def own_kernel(heads, dh, scale, q_hbm, do_hbm, l_hbm, o_hbm, kv_hbm, dq_ref, g_ref, lt_ref, ot_ref, q_ref, do_ref, l_ref, o_ref, kv_ref, kt_ref, dk_ref, dv_ref, sem):
    rows, width = q_ref.shape
    half = rows // 2
    wide = width // 2
    small = [
        pltpu.make_async_copy(a, b, sem.at[i]) for i, (a, b) in enumerate(((l_hbm, l_ref), (o_hbm, o_ref), (kv_hbm, kv_ref)))
    ]
    large = [
        [
            pltpu.make_async_copy(a.at[:, pl.ds(i * wide, wide)], b.at[:, pl.ds(i * wide, wide)], sem.at[3 + 2 * i + j])
            for j, (a, b) in enumerate(((q_hbm, q_ref), (do_hbm, do_ref)))
        ]
        for i in range(2)
    ]
    for c in small + large[0] + large[1]:
        c.start()
    dk_ref[...] = jnp.zeros_like(dk_ref)
    dv_ref[...] = jnp.zeros_like(dv_ref)
    for c in small:
        c.wait()
    lt_ref[...] = l_ref[...].astype(F32) * LOG2E
    ot_ref[...] = o_ref[...].astype(F32)
    kt_ref[...] = kv_ref[:, :dh].astype(F32).T.astype(BF16)
    key_ids = lax.broadcasted_iota(jnp.int32, (half, half), 0)
    row_ids = lax.broadcasted_iota(jnp.int32, (half, half), 1)
    visible = key_ids <= row_ids
    for h in range(heads):
        if h % (heads // 2) == 0:
            for c in large[h // (heads // 2)]:
                c.wait()
        hs = slice(h * dh, (h + 1) * dh)
        for t in range(2):
            ks = slice(t * half, (t + 1) * half)
            rs = slice(t * half, rows)
            q, do = q_ref[rs, hs], do_ref[rs, hs]
            k, v = kv_ref[ks, :dh], kv_ref[ks, dh:]
            p = jnp.exp2(dot(k, q, 1, 1) * (scale * LOG2E) - lt_ref[h : h + 1, rs])
            first = jnp.where(visible, p[:, :half], 0.0)
            p = first if t == 1 else jnp.concatenate([first, p[:, half:]], axis=1)
            ds = (p * (dot(v, do, 1, 1) - ot_ref[h : h + 1, rs])).astype(BF16)
            dk_ref[ks, :] += dot(ds, q, 1, 0)
            dv_ref[ks, :] += dot(p.astype(BF16), do, 1, 0)
            part = dot(kt_ref[:, ks], ds, 1, 0)
            if t == 0:
                dq_ref[hs, :] = part
            else:
                dq_ref[hs, rs] += part
    g_ref[:, :dh] = (dk_ref[...] * scale).astype(BF16)
    g_ref[:, dh:] = dv_ref[...].astype(BF16)


def own(q, do, totals, offsets, kv):
    rows, width = q.shape
    heads = totals.shape[0]
    dh = width // heads
    return pl.pallas_call(
        functools.partial(own_kernel, heads, dh, dh**-0.5),
        in_specs=[HBM] * 5,
        out_specs=[VMEM] * 6,
        out_shape=[
            jax.ShapeDtypeStruct((width, rows), F32),
            jax.ShapeDtypeStruct((rows, 2 * dh), BF16),
            jax.ShapeDtypeStruct((heads, rows), F32),
            jax.ShapeDtypeStruct((heads, rows), F32),
            jax.ShapeDtypeStruct((rows, width), BF16),
            jax.ShapeDtypeStruct((rows, width), BF16),
        ],
        scratch_shapes=[
            pltpu.VMEM((heads, rows), BF16),
            pltpu.VMEM((heads, rows), BF16),
            pltpu.VMEM((rows, 2 * dh), BF16),
            pltpu.VMEM((dh, rows), BF16),
            pltpu.VMEM((rows, dh), F32),
            pltpu.VMEM((rows, dh), F32),
            pltpu.SemaphoreType.DMA((7,)),
        ],
        compiler_params=params(20),
        cost_estimate=cost(rows, rows * 3 // 4, heads, dh),
        name="own",
    )(*(in_hbm(x) for x in (q, do, totals, offsets, kv)))


def piece_kernel(heads, dh, scale, block, first, *refs):
    if first:
        depth_ref, q_ref, do_ref, lt_ref, ot_ref, kv_ref, dq_ref, g_ref, kt_ref, dk_ref, dv_ref = refs
        from_ref = None
    else:
        depth_ref, q_ref, do_ref, lt_ref, ot_ref, kv_ref, from_ref, dq_ref, g_ref, kt_ref, dk_ref, dv_ref = refs

    def work():
        kt_ref[...] = kv_ref[:, :dh].astype(F32).T.astype(BF16)
        dk_ref[...] = jnp.zeros_like(dk_ref)
        dv_ref[...] = jnp.zeros_like(dv_ref)
        for h in range(heads):
            hs = slice(h * dh, (h + 1) * dh)
            q, do = q_ref[:, hs], do_ref[:, hs]
            p = jnp.exp2(dot(kv_ref[:, :dh], q, 1, 1) * (scale * LOG2E) - lt_ref[h : h + 1, :])
            ds = (p * (dot(kv_ref[:, dh:], do, 1, 1) - ot_ref[h : h + 1, :])).astype(BF16)
            dk_ref[...] += dot(ds, q, 1, 0)
            dv_ref[...] += dot(p.astype(BF16), do, 1, 0)
            part = dot(kt_ref[...], ds, 1, 0)
            dq_ref[hs, :] = part if first else from_ref[hs, :] + part
        g_ref[:, :dh] = (dk_ref[...] * scale).astype(BF16)
        g_ref[:, dh:] = dv_ref[...].astype(BF16)

    if block == 0:
        work()
    else:
        pl.when(depth_ref[0] > block)(work)


def piece(depth, q, do, lt, ot, kv, dq, block):
    rows, width = q.shape
    heads = lt.shape[0]
    dh = width // heads
    keys = kv.shape[0]
    args = (depth, q, do, lt, ot, kv) + (() if dq is None else (dq,))
    return pl.pallas_call(
        functools.partial(piece_kernel, heads, dh, dh**-0.5, block, dq is None),
        in_specs=[SMEM] + [VMEM] * (len(args) - 1),
        out_specs=[VMEM] * 2,
        out_shape=[jax.ShapeDtypeStruct((width, rows), F32), jax.ShapeDtypeStruct((keys, 2 * dh), BF16)],
        scratch_shapes=[pltpu.VMEM((dh, keys), BF16), pltpu.VMEM((keys, dh), F32), pltpu.VMEM((keys, dh), F32)],
        input_output_aliases={} if dq is None else {6: 0},
        compiler_params=params(20),
        cost_estimate=cost(rows, keys, heads, dh),
        name="piece",
    )(*args)


def join_kernel(heads, dh, scale, own_ref, pool_ref, out_ref):
    for h in range(heads):
        hs = slice(h * dh, (h + 1) * dh)
        pool_term = (pool_ref[hs, :] * scale).astype(BF16).astype(F32)
        out_ref[:, hs] = (own_ref[hs, :] * scale + pool_term).T.astype(BF16)


def join(own_dq, pool_dq, heads):
    width, rows = own_dq.shape
    dh = width // heads
    return pl.pallas_call(
        functools.partial(join_kernel, heads, dh, dh**-0.5),
        in_specs=[VMEM] * 2,
        out_specs=VMEM,
        out_shape=jax.ShapeDtypeStruct((rows, width), BF16),
        compiler_params=params(8),
        name="join",
    )(own_dq, pool_dq)


def place_kernel(rows, table_ref, *refs):
    ins, out_ref, sem = refs[: len(PIECES)], refs[-2], refs[-1]
    copies = []
    for i, (block, first, size) in enumerate(PIECES):
        at = pl.multiple_of(table_ref[block] * rows + first, 128)
        copies.append(pltpu.make_async_copy(ins[i], out_ref.at[pl.ds(at, size), :], sem.at[i]))
    for c in copies:
        c.start()
    for c in copies:
        c.wait()


def place(table, parts, shape, rows):
    return pl.pallas_call(
        functools.partial(place_kernel, rows),
        in_specs=[SMEM] + [VMEM] * len(parts),
        out_specs=HBM,
        out_shape=jax.ShapeDtypeStruct(shape, BF16),
        scratch_shapes=[pltpu.SemaphoreType.DMA((len(PIECES),))],
        compiler_params=params(4),
        name="place",
    )(table, *parts)


def per_device(query, grad_output, log_total, offset, slice_keys, pool_keys, block_table):
    rows, heads = log_total.shape[1:]
    table = block_table[0]
    sections = lax.axis_size("section")
    half_axis = sections // 2
    group = sections // NSL
    depths = [NSL - 1 - layer // group % (NSL - 1) for layer in range(sections)]
    me = lax.axis_index("section")
    depth = (NSL - 1 - me // group % (NSL - 1)).astype(jnp.int32).reshape(1)

    def pairs(block):
        return [(layer, (layer + half_axis) % sections) for layer in range(sections) if depths[layer] > block]

    picked = pick(table, pool_keys[0], rows)
    arrived = []
    for i, (block, _, _) in enumerate(PIECES):
        arrived.append(lax.ppermute(picked[i], "section", [(p, layer) for layer, p in pairs(block)]))
    own_dq, slice_grad, lt, ot, q, do = own(query[0], grad_output[0], log_total[0].T, offset[0].T, slice_keys[0])
    dq = None
    parts = []
    for i, (block, _, _) in enumerate(PIECES):
        dq, g = piece(depth, q, do, lt, ot, arrived[i], dq, block)
        parts.append(lax.ppermute(g, "section", pairs(block)))
    query_grad = join(own_dq, dq, heads)
    pool_grad = place(table, parts, pool_keys.shape[1:], rows)
    return (query_grad[None], slice_grad[None], pool_grad[None])


def solution(mesh):
    spec = P("section", None, "kv")
    return jax.shard_map(
        per_device,
        mesh=mesh,
        in_specs=(spec, spec, spec, spec, spec, spec, P("section", None)),
        out_specs=(spec, spec, spec),
        check_vma=False,
    )
```

time: 147 us -> 62 us (0.42)
  the two profiles are of different devices: /device:TPU:28 before, /device:TPU:10 now
where the time goes in v1:
time: 62 us; the launch traced here: 61.6 us
  Pallas kernels  23.1 us (37%)
  starting transfers between devices  19.4 us (31%)
  waiting for transfers between devices  13.1 us (21%)
  local copies, waits for them, and re-layouts  5.05 us (8%)
  between operations  0.91 us (1%)
    ppermute x3, waiting for transfers between devices, per_device(): parts.append(lax.ppermute(g, 'section', pairs(block)))  13.1 us
    ppermute x3, starting transfers between devices, per_device(): parts.append(lax.ppermute(g, 'section', pairs(block)))  11.9 us
    pallas_call x3, Pallas kernels, piece(): pl.pallas_call(functools.partial(piece_kernel, heads, dh, dh ** (-0.5), b...  11.2 us
    ppermute x3, starting transfers between devices, per_device(): lax.ppermute(picked[i], 'section', [(p, layer) for layer, p in pairs(bloc...  7.45 us
    pallas_call x1, Pallas kernels, own(): pl.pallas_call(functools.partial(own_kernel, heads, dh, dh ** (-0.5)), in...  7.36 us
    unnamed x12, local copies, waits for them, and re-layouts  5.05 us
    pallas_call x1, Pallas kernels, pick(): pl.pallas_call(functools.partial(pick_kernel, rows), in_specs=[SMEM, HBM]...  1.68 us
    pallas_call x1, Pallas kernels, join(): pl.pallas_call(functools.partial(join_kernel, heads, dh, dh ** (-0.5)), i...  1.5 us
  transfers between devices with their start and end apart: 6, of which 3 were waited for; matrix products, arithmetic and copies ran while one was open for 0% of the time, Pallas kernels for 32%

profile of v1, /device:TPU:10, one launch (start us, length us, event | category | flops | bytes accessed | tf_op | source)
XLA Modules:
  0.0 61.6 jit_solution(14105837120857137354)
XLA Ops:
  0.6 0.0 copy-start
  0.6 0.6 %copy-done = s32[1,3]{1,0:T(1,128)S(1)} copy-done((s32[1,3]{1,0:T(1,128)S(1)}, s32[1,3]{1,0:T(1,128)}, u32[]{:S(2)}) %copy-start) | copy-done | bytes 36
  1.3 1.7 %pick.1 = (bf16[512,256]{1,0:T(8,128)(2,1)S(1)}, bf16[512,256]{1,0:T(8,128)(2,1)S(1)}, bf16[512,256]{1,0:T(8,128)(2,1)S(1)}) custom-call(s32[3]{0:T(128)S(1)} %bitcast.15, bf16[1536,256]{1,0:T(8,128)(2,1)} %bitcast.19), custom_call_target="tpu_custom_call" | custom-call | tf_op jit(solution)/shard_map/pick/pallas_call | solution.py:53
  3.0 2.2 %collective-permute-start.2 = (bf16[512,256]{1,0:T(8,128)(2,1)S(1)}, bf16[512,256]{1,0:T(8,128)(2,1)S(1)}, u32[]{:S(2)}, u32[]{:S(2)}) collective-permute-start(bf16[512,256]{1,0:T(8,128)(2,1)S(1)} %get-tuple-element.25), channel_id=1, source_target_pairs={{128,0},{132,4},{136,8},{140,12},{144,16},{148,20},{152,24},{156,2... | collective-permute-start | bytes 786440 | tf_op jit(solution)/shard_map/ppermute | solution.py:254
  5.2 3.3 %collective-permute-start = (bf16[512,256]{1,0:T(8,128)(2,1)S(1)}, bf16[512,256]{1,0:T(8,128)(2,1)S(1)}, u32[]{:S(2)}, u32[]{:S(2)}) collective-permute-start(bf16[512,256]{1,0:T(8,128)(2,1)S(1)} %get-tuple-element.23), channel_id=1, source_target_pairs={{128,0},{132,4},{136,8},{140,12},{144,16},{148,20},{152,24},{156,2... | collective-permute-start | bytes 786440 | tf_op jit(solution)/shard_map/ppermute | solution.py:254
  8.5 1.9 %collective-permute-start.1 = (bf16[512,256]{1,0:T(8,128)(2,1)S(1)}, bf16[512,256]{1,0:T(8,128)(2,1)}, u32[]{:S(2)}, u32[]{:S(2)}) collective-permute-start(bf16[512,256]{1,0:T(8,128)(2,1)S(1)} %get-tuple-element.24), channel_id=1, source_target_pairs={{128,0},{132,4},{136,8},{140,12},{144,16},{148,20},{152,24},{156,2... | collective-permute-start | bytes 786440 | tf_op jit(solution)/shard_map/ppermute | solution.py:254
  10.4 7.4 %own.1 = (f32[1024,512]{1,0:T(8,128)S(1)}, bf16[512,256]{1,0:T(8,128)(2,1)}, f32[8,512]{1,0:T(8,128)S(1)}, f32[8,512]{1,0:T(8,128)S(1)}, bf16[512,1024]{1,0:T(8,128)(2,1)S(1)}, /*index=5*/bf16[512,1024]{1,0:T(8,128)(2,1)S(1)}) custom-call(bf16[512,1024]{1,0:T(8,128)(2,1)} %bitcast.20, bf16[512,1024]{1,0:T(8,128)(2,1)} %bitcast.21, bf16[8,512]{1,0:T(8,128)(2,1)} %bitcast.23, ...), custom_call_target="tpu_custom_call" | custom-call | flops 2013265920 | bytes 1048576 | tf_op jit(solution)/shard_map/own/pallas_call | solution.py:119
  17.8 0.0 copy-start.2
  17.8 1.0 %copy-done.2 = bf16[512,1024]{1,0:T(8,128)(2,1)} copy-done((bf16[512,1024]{1,0:T(8,128)(2,1)}, bf16[512,1024]{1,0:T(8,128)(2,1)S(1)}, u32[]{:S(2)}) %copy-start.2) | copy-done | bytes 1048600
  18.8 0.0 copy-start.4
  18.8 1.0 %copy-done.4 = bf16[512,1024]{1,0:T(8,128)(2,1)} copy-done((bf16[512,1024]{1,0:T(8,128)(2,1)}, bf16[512,1024]{1,0:T(8,128)(2,1)S(1)}, u32[]{:S(2)}) %copy-start.4) | copy-done | bytes 1048600
  19.7 0.0 collective-permute-done.2.refs_5_
  19.8 0.0 copy-start.3
  19.8 1.2 %copy-done.3 = bf16[512,1024]{1,0:T(8,128)(2,1)S(1)} copy-done((bf16[512,1024]{1,0:T(8,128)(2,1)S(1)}, bf16[512,1024]{1,0:T(8,128)(2,1)}, u32[]{:S(2)}) %copy-start.3) | copy-done | bytes 1048600
  21.0 0.0 copy-start.5
  21.0 1.2 %copy-done.5 = bf16[512,1024]{1,0:T(8,128)(2,1)S(1)} copy-done((bf16[512,1024]{1,0:T(8,128)(2,1)S(1)}, bf16[512,1024]{1,0:T(8,128)(2,1)}, u32[]{:S(2)}) %copy-start.5) | copy-done | bytes 1048600
  22.2 5.1 %piece.3 = (f32[1024,512]{1,0:T(8,128)S(1)}, bf16[512,256]{1,0:T(8,128)(2,1)S(1)}) custom-call(s32[1]{0:T(128)} %bitcast.7.refs_0_, bf16[512,1024]{1,0:T(8,128)(2,1)S(1)} %copy-done.3, bf16[512,1024]{1,0:T(8,128)(2,1)S(1)} %copy-done.5, f32[8,512]{1,0:T(8,128)S(1)} %get-tuple-element.21.refs_3_, f32[8,512]{1,0:T(8,128)S(1)} %get-tuple-element.22.refs_4_, ...), custom_call_target="tpu_custom_call" | custom-call | flops 2684354560 | bytes 1048576 | tf_op jit(solution)/shard_map/piece/pallas_call | solution.py:181
  27.3 0.0 collective-permute-done.1.refs_5_
  27.3 6.1 %piece.4 = (f32[1024,512]{1,0:T(8,128)S(1)}, bf16[512,256]{1,0:T(8,128)(2,1)S(1)}) custom-call(s32[1]{0:T(128)} %bitcast.7.refs_0_, bf16[512,1024]{1,0:T(8,128)(2,1)S(1)} %copy-done.3, bf16[512,1024]{1,0:T(8,128)(2,1)S(1)} %copy-done.5, f32[8,512]{1,0:T(8,128)S(1)} %get-tuple-element.21.refs_3_, ...), custom_call_target="tpu_custom_call", output_to_operand_aliasing={{0}: (6, {})} | custom-call | flops 2684354560 | bytes 1048576 | tf_op jit(solution)/shard_map/piece/pallas_call | solution.py:181
  33.4 0.0 collective-permute-done.refs_5_
  33.4 1.3 %collective-permute-start.5 = (bf16[512,256]{1,0:T(8,128)(2,1)S(1)}, bf16[512,256]{1,0:T(8,128)(2,1)S(1)}, u32[]{:S(2)}, u32[]{:S(2)}) collective-permute-start(bf16[512,256]{1,0:T(8,128)(2,1)S(1)} %get-tuple-element.32), channel_id=1, source_target_pairs={{0,128},{4,132},{8,136},{12,140},{16,144},{20,148},{24,152},{28,15... | collective-permute-start | bytes 786440 | tf_op jit(solution)/shard_map/ppermute | solution.py:260
  34.7 10.6 %collective-permute-start.4 = (bf16[512,256]{1,0:T(8,128)(2,1)S(1)}, bf16[512,256]{1,0:T(8,128)(2,1)S(1)}, u32[]{:S(2)}, u32[]{:S(2)}) collective-permute-start(bf16[512,256]{1,0:T(8,128)(2,1)S(1)} %get-tuple-element.31), channel_id=1, source_target_pairs={{0,128},{4,132},{8,136},{12,140},{16,144},{20,148},{24,152},{28,15... | collective-permute-start | bytes 786440 | tf_op jit(solution)/shard_map/ppermute | solution.py:260
  45.3 0.1 collective-permute-start.3
  45.4 0.0 copy-start.1
  45.4 1.5 %join.1 = bf16[512,1024]{1,0:T(8,128)(2,1)} custom-call(f32[1024,512]{1,0:T(8,128)S(1)} %get-tuple-element.18.own_ref, f32[1024,512]{1,0:T(8,128)S(1)} %get-tuple-element.28.pool_ref), custom_call_target="tpu_custom_call" | custom-call | tf_op jit(solution)/shard_map/join/pallas_call | solution.py:204
  46.9 3.6 %collective-permute-done.5.refs_2_ = bf16[512,256]{1,0:T(8,128)(2,1)S(1)} collective-permute-done((bf16[512,256]{1,0:T(8,128)(2,1)S(1)}, bf16[512,256]{1,0:T(8,128)(2,1)S(1)}, u32[]{:S(2)}, u32[]{:S(2)}) %collective-permute-start.5) | collective-permute-done | bytes 262176 | tf_op jit(solution)/shard_map/ppermute | solution.py:260
  50.5 5.6 %collective-permute-done.4.refs_1_ = bf16[512,256]{1,0:T(8,128)(2,1)S(1)} collective-permute-done((bf16[512,256]{1,0:T(8,128)(2,1)S(1)}, bf16[512,256]{1,0:T(8,128)(2,1)S(1)}, u32[]{:S(2)}, u32[]{:S(2)}) %collective-permute-start.4) | collective-permute-done | bytes 262176 | tf_op jit(solution)/shard_map/ppermute | solution.py:260
  56.1 3.9 %collective-permute-done.3.refs_0_ = bf16[512,256]{1,0:T(8,128)(2,1)S(1)} collective-permute-done((bf16[512,256]{1,0:T(8,128)(2,1)S(1)}, bf16[512,256]{1,0:T(8,128)(2,1)S(1)}, u32[]{:S(2)}, u32[]{:S(2)}) %collective-permute-start.3) | collective-permute-done | bytes 262176 | tf_op jit(solution)/shard_map/ppermute | solution.py:260
  60.0 0.0 copy-done.1
  60.0 1.4 %place.1 = bf16[1536,256]{1,0:T(8,128)(2,1)} custom-call(s32[3]{0:T(128)S(1)} %bitcast.16, bf16[512,256]{1,0:T(8,128)(2,1)S(1)} %collective-permute-done.3.refs_0_, bf16[512,256]{1,0:T(8,128)(2,1)S(1)} %collective-permute-done.4.refs_1_, bf16[512,256]{1,0:T(8,128)(2,1)S(1)} %collective-permute-done.5.refs_2_), custom_call_target="tpu_custom_call" | custom-call | tf_op jit(solution)/shard_map/place/pallas_call | solution.py:227
  (1 shorter events, 0.0 us)
Async XLA Ops:
  0.6 0.7 %copy-start = (s32[1,3]{1,0:T(1,128)S(1)}, s32[1,3]{1,0:T(1,128)}, u32[]{:S(2)}) copy-start(s32[1,3]{1,0:T(1,128)} %param.13) | copy-start | bytes 40
  3.0 16.8 %collective-permute-start.2 = (bf16[512,256]{1,0:T(8,128)(2,1)S(1)}, bf16[512,256]{1,0:T(8,128)(2,1)S(1)}, u32[]{:S(2)}, u32[]{:S(2)}) collective-permute-start(bf16[512,256]{1,0:T(8,128)(2,1)S(1)} %get-tuple-element.25), channel_id=1, source_target_pairs={{128,0},{132,4},{136,8},{140,12},{144,16},{148,20},{152,24},{156,2... | collective-permute-start | bytes 786440 | tf_op jit(solution)/shard_map/ppermute | solution.py:254
  5.2 28.2 %collective-permute-start = (bf16[512,256]{1,0:T(8,128)(2,1)S(1)}, bf16[512,256]{1,0:T(8,128)(2,1)S(1)}, u32[]{:S(2)}, u32[]{:S(2)}) collective-permute-start(bf16[512,256]{1,0:T(8,128)(2,1)S(1)} %get-tuple-element.23), channel_id=1, source_target_pairs={{128,0},{132,4},{136,8},{140,12},{144,16},{148,20},{152,24},{156,2... | collective-permute-start | bytes 786440 | tf_op jit(solution)/shard_map/ppermute | solution.py:254
  8.5 18.8 %collective-permute-start.1 = (bf16[512,256]{1,0:T(8,128)(2,1)S(1)}, bf16[512,256]{1,0:T(8,128)(2,1)}, u32[]{:S(2)}, u32[]{:S(2)}) collective-permute-start(bf16[512,256]{1,0:T(8,128)(2,1)S(1)} %get-tuple-element.24), channel_id=1, source_target_pairs={{128,0},{132,4},{136,8},{140,12},{144,16},{148,20},{152,24},{156,2... | collective-permute-start | bytes 786440 | tf_op jit(solution)/shard_map/ppermute | solution.py:254
  17.8 1.0 %copy-start.2 = (bf16[512,1024]{1,0:T(8,128)(2,1)}, bf16[512,1024]{1,0:T(8,128)(2,1)S(1)}, u32[]{:S(2)}) copy-start(bf16[512,1024]{1,0:T(8,128)(2,1)S(1)} %get-tuple-element.19.refs_1_) | copy-start | bytes 3145732
  18.8 1.0 %copy-start.4 = (bf16[512,1024]{1,0:T(8,128)(2,1)}, bf16[512,1024]{1,0:T(8,128)(2,1)S(1)}, u32[]{:S(2)}) copy-start(bf16[512,1024]{1,0:T(8,128)(2,1)S(1)} %get-tuple-element.20.refs_2_) | copy-start | bytes 3145732
  19.8 1.2 %copy-start.3 = (bf16[512,1024]{1,0:T(8,128)(2,1)S(1)}, bf16[512,1024]{1,0:T(8,128)(2,1)}, u32[]{:S(2)}) copy-start(bf16[512,1024]{1,0:T(8,128)(2,1)} %copy-done.2) | copy-start | bytes 3145732
  21.0 1.2 %copy-start.5 = (bf16[512,1024]{1,0:T(8,128)(2,1)S(1)}, bf16[512,1024]{1,0:T(8,128)(2,1)}, u32[]{:S(2)}) copy-start(bf16[512,1024]{1,0:T(8,128)(2,1)} %copy-done.4) | copy-start | bytes 3145732
  33.4 17.1 %collective-permute-start.5 = (bf16[512,256]{1,0:T(8,128)(2,1)S(1)}, bf16[512,256]{1,0:T(8,128)(2,1)S(1)}, u32[]{:S(2)}, u32[]{:S(2)}) collective-permute-start(bf16[512,256]{1,0:T(8,128)(2,1)S(1)} %get-tuple-element.32), channel_id=1, source_target_pairs={{0,128},{4,132},{8,136},{12,140},{16,144},{20,148},{24,152},{28,15... | collective-permute-start | bytes 786440 | tf_op jit(solution)/shard_map/ppermute | solution.py:260
  34.7 21.4 %collective-permute-start.4 = (bf16[512,256]{1,0:T(8,128)(2,1)S(1)}, bf16[512,256]{1,0:T(8,128)(2,1)S(1)}, u32[]{:S(2)}, u32[]{:S(2)}) collective-permute-start(bf16[512,256]{1,0:T(8,128)(2,1)S(1)} %get-tuple-element.31), channel_id=1, source_target_pairs={{0,128},{4,132},{8,136},{12,140},{16,144},{20,148},{24,152},{28,15... | collective-permute-start | bytes 786440 | tf_op jit(solution)/shard_map/ppermute | solution.py:260
  45.3 14.8 %collective-permute-start.3 = (bf16[512,256]{1,0:T(8,128)(2,1)S(1)}, bf16[512,256]{1,0:T(8,128)(2,1)S(1)}, u32[]{:S(2)}, u32[]{:S(2)}) collective-permute-start(bf16[512,256]{1,0:T(8,128)(2,1)S(1)} %get-tuple-element.30), channel_id=1, source_target_pairs={{0,128},{4,132},{8,136},{12,140},{16,144},{20,148},{24,152},{28,15... | collective-permute-start | bytes 786440 | tf_op jit(solution)/shard_map/ppermute | solution.py:260
  45.4 14.7 %copy-start.1 = (s32[1,3]{1,0:T(1,128)S(1)}, s32[1,3]{1,0:T(1,128)}, u32[]{:S(2)}) copy-start(s32[1,3]{1,0:T(1,128)} %param.13) | copy-start | bytes 40

commit v2 on v1

v2 whole, which is shorter than its diff:
```python
import functools

import jax
import jax.numpy as jnp
from jax import lax
from jax.experimental import pallas as pl
from jax.experimental.pallas import tpu as pltpu
from jax.sharding import PartitionSpec as P


NSL = 4
LOG2E = 1.4426950408889634
F32 = jnp.float32
BF16 = jnp.bfloat16
VMEM = pl.BlockSpec(memory_space=pltpu.VMEM)
SMEM = pl.BlockSpec(memory_space=pltpu.SMEM)
HBM = pl.BlockSpec(memory_space=pltpu.HBM)
PIECES = ((0, 0, 512), (2, 0, 512), (1, 0, 512))


def dot(a, b, ca, cb):
    return lax.dot_general(a, b, (((ca,), (cb,)), ((), ())), preferred_element_type=F32)


def in_hbm(x):
    return pltpu.with_memory_space_constraint(x, pltpu.HBM)


def params(mib):
    return pltpu.CompilerParams(vmem_limit_bytes=mib << 20)


def cost(rows, keys, heads, dh):
    return pl.CostEstimate(
        flops=10 * rows * keys * heads * dh, bytes_accessed=1 << 20, transcendentals=rows * keys * heads
    )


def pick_kernel(rows, table_ref, pool_ref, *refs):
    outs, sem = refs[:-1], refs[-1]
    copies = []
    for i, (block, first, size) in enumerate(PIECES):
        at = pl.multiple_of(table_ref[block] * rows + first, 128)
        copies.append(pltpu.make_async_copy(pool_ref.at[pl.ds(at, size), :], outs[i], sem.at[i]))
    for c in copies:
        c.start()
    for c in copies:
        c.wait()


def pick(table, pool, rows):
    width = pool.shape[1]
    return pl.pallas_call(
        functools.partial(pick_kernel, rows),
        in_specs=[SMEM, HBM],
        out_specs=[VMEM] * len(PIECES),
        out_shape=[jax.ShapeDtypeStruct((size, width), pool.dtype) for _, _, size in PIECES],
        scratch_shapes=[pltpu.SemaphoreType.DMA((len(PIECES),))],
        compiler_params=params(4),
        name="pick",
    )(table, in_hbm(pool))


def prep_kernel(heads, dh, q_hbm, do_hbm, l_hbm, o_hbm, q_ref, do_ref, qt_ref, dot_ref, l_ref, o_ref, lraw_ref, oraw_ref, sem):
    rows = lraw_ref.shape[1]
    half = rows // 2
    small = [pltpu.make_async_copy(l_hbm, lraw_ref, sem.at[0]), pltpu.make_async_copy(o_hbm, oraw_ref, sem.at[1])]
    large = []
    for t in range(2):
        for h in range(heads):
            at = (t * heads + h) * half
            for a, b in ((q_hbm, q_ref), (do_hbm, do_ref)):
                large.append(
                    pltpu.make_async_copy(
                        a.at[pl.ds(t * half, half), pl.ds(h * dh, dh)], b.at[pl.ds(at, half), :], sem.at[2 + len(large)]
                    )
                )
    for c in small + large:
        c.start()
    for c in small:
        c.wait()
    lcol = (lraw_ref[...].astype(F32) * LOG2E).T
    ocol = oraw_ref[...].astype(F32).T
    for t in range(2):
        for h in range(heads):
            part = slice((t * heads + h) * half, (t * heads + h + 1) * half)
            l_ref[part, :] = jnp.broadcast_to(lcol[t * half : (t + 1) * half, h : h + 1], (half, dh))
            o_ref[part, :] = jnp.broadcast_to(ocol[t * half : (t + 1) * half, h : h + 1], (half, dh))
    for i in range(2 * heads):
        part = slice(i * half, (i + 1) * half)
        large[2 * i].wait()
        qt_ref[:, part] = q_ref[part, :].T
        large[2 * i + 1].wait()
        dot_ref[:, part] = do_ref[part, :].T


def prep(q, do, totals, offsets):
    rows, width = q.shape
    heads = totals.shape[0]
    dh = width // heads
    many = heads * rows
    return pl.pallas_call(
        functools.partial(prep_kernel, heads, dh),
        in_specs=[HBM] * 4,
        out_specs=[VMEM] * 6,
        out_shape=[
            jax.ShapeDtypeStruct((many, dh), BF16),
            jax.ShapeDtypeStruct((many, dh), BF16),
            jax.ShapeDtypeStruct((dh, many), BF16),
            jax.ShapeDtypeStruct((dh, many), BF16),
            jax.ShapeDtypeStruct((many, dh), F32),
            jax.ShapeDtypeStruct((many, dh), F32),
        ],
        scratch_shapes=[
            pltpu.VMEM((heads, rows), BF16),
            pltpu.VMEM((heads, rows), BF16),
            pltpu.SemaphoreType.DMA((2 + 4 * heads,)),
        ],
        compiler_params=params(16),
        cost_estimate=pl.CostEstimate(flops=1000, bytes_accessed=4 << 20, transcendentals=0),
        name="prep",
    )(*(in_hbm(x) for x in (q, do, totals, offsets)))


def own_kernel(heads, scale, q_ref, do_ref, qt_ref, dot_ref, l_ref, o_ref, kv_ref, pool_ref, out_ref, g_ref, dk_ref, dv_ref):
    many, dh = q_ref.shape
    half = many // heads // 2
    step = many // 4
    key_ids = lax.broadcasted_iota(jnp.int32, (step, half), 1)
    row_ids = lax.rem(lax.broadcasted_iota(jnp.int32, (step, half), 0), half)
    visible = key_ids <= row_ids
    k, v = kv_ref[:, :dh], kv_ref[:, dh:]
    for c in (2, 3, 0, 1):
        t = c // 2
        rs = slice(c * step, (c + 1) * step)
        keys = (t + 1) * half
        over = keys // dh
        s = dot(q_ref[rs, :], k[:keys], 1, 1)
        dp = dot(do_ref[rs, :], v[:keys], 1, 1)
        p = jnp.exp2(s * (scale * LOG2E) - jnp.concatenate([l_ref[rs, :]] * over, axis=1))
        last = jnp.where(visible, p[:, keys - half :], 0.0)
        p = last if t == 0 else jnp.concatenate([p[:, :half], last], axis=1)
        ds = (p * (dp - jnp.concatenate([o_ref[rs, :]] * over, axis=1))).astype(BF16)
        dq = dot(ds, k[:keys], 1, 0)
        for i in range(heads // 2):
            h = (c % 2) * (heads // 2) + i
            pool_term = (pool_ref[c * step + i * half : c * step + (i + 1) * half, :] * scale).astype(BF16).astype(F32)
            total = dq[i * half : (i + 1) * half, :] * scale + pool_term
            out_ref[t * half : (t + 1) * half, h * dh : (h + 1) * dh] = total.astype(BF16)
        dk = dot(qt_ref[:, rs], ds, 1, 0)
        dv = dot(dot_ref[:, rs], p.astype(BF16), 1, 0)
        if c == 2:
            dk_ref[...] = dk
            dv_ref[...] = dv
        else:
            dk_ref[:, :keys] += dk
            dv_ref[:, :keys] += dv
    g_ref[:, :dh] = (dk_ref[...].T * scale).astype(BF16)
    g_ref[:, dh:] = dv_ref[...].T.astype(BF16)


def own(rows_of, kv, pool_dq):
    many, dh = pool_dq.shape
    rows = kv.shape[0]
    heads = many // rows
    return pl.pallas_call(
        functools.partial(own_kernel, heads, dh**-0.5),
        in_specs=[VMEM] * 8,
        out_specs=[VMEM] * 2,
        out_shape=[jax.ShapeDtypeStruct((rows, heads * dh), BF16), jax.ShapeDtypeStruct((rows, 2 * dh), BF16)],
        scratch_shapes=[pltpu.VMEM((dh, rows), F32), pltpu.VMEM((dh, rows), F32)],
        compiler_params=params(24),
        cost_estimate=cost(many, rows * 3 // 4, 1, dh),
        name="own",
    )(*rows_of, kv, pool_dq)


def piece_kernel(step, scale, block, first, *refs):
    if first:
        depth_ref, q_ref, do_ref, qt_ref, dot_ref, l_ref, o_ref, kv_ref, dq_ref, g_ref, dk_ref, dv_ref = refs
    else:
        depth_ref, q_ref, do_ref, qt_ref, dot_ref, l_ref, o_ref, kv_ref, from_ref, dq_ref, g_ref, dk_ref, dv_ref = refs
    many, dh = q_ref.shape
    over = kv_ref.shape[0] // dh

    def work():
        k, v = kv_ref[:, :dh], kv_ref[:, dh:]
        for c in range(many // step):
            rs = slice(c * step, (c + 1) * step)
            s = dot(q_ref[rs, :], k, 1, 1)
            dp = dot(do_ref[rs, :], v, 1, 1)
            p = jnp.exp2(s * (scale * LOG2E) - jnp.concatenate([l_ref[rs, :]] * over, axis=1))
            ds = (p * (dp - jnp.concatenate([o_ref[rs, :]] * over, axis=1))).astype(BF16)
            part = dot(ds, k, 1, 0)
            dq_ref[rs, :] = part if first else from_ref[rs, :] + part
            dk = dot(qt_ref[:, rs], ds, 1, 0)
            dv = dot(dot_ref[:, rs], p.astype(BF16), 1, 0)
            if c == 0:
                dk_ref[...] = dk
                dv_ref[...] = dv
            else:
                dk_ref[...] += dk
                dv_ref[...] += dv
        g_ref[:, :dh] = (dk_ref[...].T * scale).astype(BF16)
        g_ref[:, dh:] = dv_ref[...].T.astype(BF16)

    if block == 0:
        work()
        return
    pl.when(depth_ref[0] > block)(work)

    @pl.when(depth_ref[0] <= block)
    def _():
        g_ref[...] = jnp.zeros_like(g_ref)


def piece(depth, rows_of, kv, dq, block):
    many, dh = rows_of[0].shape
    keys = kv.shape[0]
    args = (depth, *rows_of, kv) + (() if dq is None else (dq,))
    return pl.pallas_call(
        functools.partial(piece_kernel, many // 4, dh**-0.5, block, dq is None),
        in_specs=[SMEM] + [VMEM] * (len(args) - 1),
        out_specs=[VMEM] * 2,
        out_shape=[jax.ShapeDtypeStruct((many, dh), F32), jax.ShapeDtypeStruct((keys, 2 * dh), BF16)],
        scratch_shapes=[pltpu.VMEM((dh, keys), F32), pltpu.VMEM((dh, keys), F32)],
        input_output_aliases={} if dq is None else {8: 0},
        compiler_params=params(24),
        cost_estimate=cost(many, keys, 1, dh),
        name="piece",
    )(*args)


def place_kernel(rows, table_ref, *refs):
    ins, out_ref, sem = refs[: len(PIECES)], refs[-2], refs[-1]
    copies = []
    for i, (block, first, size) in enumerate(PIECES):
        at = pl.multiple_of(table_ref[block] * rows + first, 128)
        copies.append(pltpu.make_async_copy(ins[i], out_ref.at[pl.ds(at, size), :], sem.at[i]))
    for c in copies:
        c.start()
    for c in copies:
        c.wait()


def place(table, parts, shape, rows):
    return pl.pallas_call(
        functools.partial(place_kernel, rows),
        in_specs=[SMEM] + [VMEM] * len(parts),
        out_specs=HBM,
        out_shape=jax.ShapeDtypeStruct(shape, BF16),
        scratch_shapes=[pltpu.SemaphoreType.DMA((len(PIECES),))],
        compiler_params=params(4),
        name="place",
    )(table, *parts)


def per_device(query, grad_output, log_total, offset, slice_keys, pool_keys, block_table):
    rows, _ = log_total.shape[1:]
    table = block_table[0]
    sections = lax.axis_size("section")
    half_axis = sections // 2
    group = sections // NSL
    depths = [NSL - 1 - layer // group % (NSL - 1) for layer in range(sections)]
    me = lax.axis_index("section")
    depth = (NSL - 1 - me // group % (NSL - 1)).astype(jnp.int32).reshape(1)

    swap = [(layer, (layer + half_axis) % sections) for layer in range(sections)]
    deep = [(p, layer) for layer, p in swap if depths[layer] == NSL - 1]

    picked = pick(table, pool_keys[0], rows)
    arrived = []
    for i, (block, _, _) in enumerate(PIECES):
        arrived.append(lax.ppermute(picked[i], "section", deep if block == NSL - 2 else swap))
    rows_of = prep(query[0], grad_output[0], log_total[0].T, offset[0].T)
    dq = None
    parts = []
    for i, (block, _, _) in enumerate(PIECES):
        dq, g = piece(depth, rows_of, arrived[i], dq, block)
        parts.append(lax.ppermute(g, "section", swap))
    query_grad, slice_grad = own(rows_of, slice_keys[0], dq)
    pool_grad = place(table, parts, pool_keys.shape[1:], rows)
    return (query_grad[None], slice_grad[None], pool_grad[None])


def solution(mesh):
    spec = P("section", None, "kv")
    return jax.shard_map(
        per_device,
        mesh=mesh,
        in_specs=(spec, spec, spec, spec, spec, spec, P("section", None)),
        out_specs=(spec, spec, spec),
        check_vma=False,
    )
```

time: 62 us -> 65.5 us (1.056)
  the two profiles are of different devices: /device:TPU:10 before, /device:TPU:8 now
where the time goes in v2:
time: 65.5 us; the launch traced here: 65.1 us
  Pallas kernels  29.4 us (45%)
  starting transfers between devices  13 us (20%)
  waiting for transfers between devices  11.7 us (18%)
  local copies, waits for them, and re-layouts  10.2 us (16%)
  between operations  0.92 us (1%)
    pallas_call x3, Pallas kernels, piece(): pl.pallas_call(functools.partial(piece_kernel, many // 4, dh ** (-0.5), b...  16.3 us
    ppermute x3, waiting for transfers between devices, per_device(): parts.append(lax.ppermute(g, 'section', swap))  11.7 us
    unnamed x22, local copies, waits for them, and re-layouts  10.2 us
    ppermute x3, starting transfers between devices, per_device(): lax.ppermute(picked[i], 'section', deep if block == NSL - 2 else swap)  9.26 us
    pallas_call x1, Pallas kernels, own(): pl.pallas_call(functools.partial(own_kernel, heads, dh ** (-0.5)), in_spe...  4.64 us
    pallas_call x1, Pallas kernels, prep(): pl.pallas_call(functools.partial(prep_kernel, heads, dh), in_specs=[HBM]...  4.38 us
    ppermute x3, starting transfers between devices, per_device(): parts.append(lax.ppermute(g, 'section', swap))  3.71 us
    pallas_call x1, Pallas kernels, pick(): pl.pallas_call(functools.partial(pick_kernel, rows), in_specs=[SMEM, HBM]...  2.57 us
  transfers between devices with their start and end apart: 6, of which 3 were waited for; matrix products, arithmetic and copies ran while one was open for 0% of the time, Pallas kernels for 31%

profile of v2, /device:TPU:8, one launch (start us, length us, event | category | flops | bytes accessed | tf_op | source)
XLA Modules:
  0.0 65.1 jit_solution(6681771076255001097)
XLA Ops:
  0.6 0.0 copy-start.9
  0.6 0.6 copy-done.9
  1.3 2.6 %pick.1 = (bf16[512,256]{1,0:T(8,128)(2,1)}, bf16[512,256]{1,0:T(8,128)(2,1)}, bf16[512,256]{1,0:T(8,128)(2,1)}) custom-call(s32[3]{0:T(128)S(1)} %bitcast.16, bf16[1536,256]{1,0:T(8,128)(2,1)} %bitcast.21), custom_call_target="tpu_custom_call" | custom-call | tf_op jit(solution)/shard_map/pick/pallas_call | solution.py:53
  3.9 3.1 %collective-permute-start.2 = (bf16[512,256]{1,0:T(8,128)(2,1)}, bf16[512,256]{1,0:T(8,128)(2,1)}, u32[]{:S(2)}, u32[]{:S(2)}) collective-permute-start(bf16[512,256]{1,0:T(8,128)(2,1)} %get-tuple-element.28), channel_id=1, source_target_pairs={{0,128},{4,132},{8,136},{12,140},{16,144},{20,148},{24,152},{28,15... | collective-permute-start | bytes 786440 | tf_op jit(solution)/shard_map/ppermute | solution.py:274
  7.0 1.3 %collective-permute-start.1 = (bf16[512,256]{1,0:T(8,128)(2,1)}, bf16[512,256]{1,0:T(8,128)(2,1)}, u32[]{:S(2)}, u32[]{:S(2)}) collective-permute-start(bf16[512,256]{1,0:T(8,128)(2,1)} %get-tuple-element.27), channel_id=1, source_target_pairs={{128,0},{132,4},{136,8},{140,12},{144,16},{148,20},{152,24},{156,2... | collective-permute-start | bytes 786440 | tf_op jit(solution)/shard_map/ppermute | solution.py:274
  8.3 4.9 %collective-permute-start = (bf16[512,256]{1,0:T(8,128)(2,1)}, bf16[512,256]{1,0:T(8,128)(2,1)S(1)}, u32[]{:S(2)}, u32[]{:S(2)}) collective-permute-start(bf16[512,256]{1,0:T(8,128)(2,1)} %get-tuple-element.26), channel_id=1, source_target_pairs={{0,128},{4,132},{8,136},{12,140},{16,144},{20,148},{24,152},{28,15... | collective-permute-start | bytes 786440 | tf_op jit(solution)/shard_map/ppermute | solution.py:274
  13.1 4.4 %prep.1 = (bf16[4096,128]{1,0:T(8,128)(2,1)S(1)}, bf16[4096,128]{1,0:T(8,128)(2,1)S(1)}, bf16[128,4096]{1,0:T(8,128)(2,1)S(1)}, bf16[128,4096]{1,0:T(8,128)(2,1)...) custom-call(bf16[512,1024]{1,0:T(8,128)(2,1)} %bitcast.18, bf16[512,1024]{1,0:T(8,128)(2,1)} %bitcast.19, ...), custom_call_target="tpu_custom_call" | custom-call | flops 1000 | bytes 4194304 | tf_op jit(solution)/shard_map/prep/pallas_call | solution.py:102
  17.5 0.0 copy-start
  17.5 1.3 %copy-done = f32[4096,128]{1,0:T(8,128)} copy-done((f32[4096,128]{1,0:T(8,128)}, f32[4096,128]{1,0:T(8,128)S(1)}, u32[]{:S(2)}) %copy-start) | copy-done | bytes 2097176
  18.9 0.0 copy-start.2
  18.9 1.0 %copy-done.2 = bf16[4096,128]{1,0:T(8,128)(2,1)} copy-done((bf16[4096,128]{1,0:T(8,128)(2,1)}, bf16[4096,128]{1,0:T(8,128)(2,1)S(1)}, u32[]{:S(2)}) %copy-start.2) | copy-done | bytes 1048600
  19.8 0.0 copy-start.4
  19.8 1.0 %copy-done.4 = bf16[128,4096]{1,0:T(8,128)(2,1)} copy-done((bf16[128,4096]{1,0:T(8,128)(2,1)}, bf16[128,4096]{1,0:T(8,128)(2,1)S(1)}, u32[]{:S(2)}) %copy-start.4) | copy-done | bytes 1048600
  20.8 0.0 copy-start.6
  20.8 1.0 %copy-done.6 = bf16[128,4096]{1,0:T(8,128)(2,1)} copy-done((bf16[128,4096]{1,0:T(8,128)(2,1)}, bf16[128,4096]{1,0:T(8,128)(2,1)S(1)}, u32[]{:S(2)}) %copy-start.6) | copy-done | bytes 1048600
  21.8 0.0 collective-permute-done.2.refs_7_
  21.8 0.0 copy-start.1
  21.8 1.6 %copy-done.1 = f32[4096,128]{1,0:T(8,128)S(1)} copy-done((f32[4096,128]{1,0:T(8,128)S(1)}, f32[4096,128]{1,0:T(8,128)}, u32[]{:S(2)}) %copy-start.1) | copy-done | bytes 2097176
  23.4 0.0 copy-start.3
  23.4 1.2 %copy-done.3 = bf16[4096,128]{1,0:T(8,128)(2,1)S(1)} copy-done((bf16[4096,128]{1,0:T(8,128)(2,1)S(1)}, bf16[4096,128]{1,0:T(8,128)(2,1)}, u32[]{:S(2)}) %copy-start.3) | copy-done | bytes 1048600
  24.6 0.0 copy-start.5
  24.6 1.2 %copy-done.5 = bf16[128,4096]{1,0:T(8,128)(2,1)S(1)} copy-done((bf16[128,4096]{1,0:T(8,128)(2,1)S(1)}, bf16[128,4096]{1,0:T(8,128)(2,1)}, u32[]{:S(2)}) %copy-start.5) | copy-done | bytes 1048600
  25.8 0.0 copy-start.7
  25.8 1.2 %copy-done.7 = bf16[128,4096]{1,0:T(8,128)(2,1)S(1)} copy-done((bf16[128,4096]{1,0:T(8,128)(2,1)S(1)}, bf16[128,4096]{1,0:T(8,128)(2,1)}, u32[]{:S(2)}) %copy-start.7) | copy-done | bytes 1048600
  27.1 5.7 %piece.3 = (f32[4096,128]{1,0:T(8,128)S(1)}, bf16[512,256]{1,0:T(8,128)(2,1)S(1)}) custom-call(s32[1]{0:T(128)} %bitcast.7.refs_0_, bf16[4096,128]{1,0:T(8,128)(2,1)S(1)} %get-tuple-element.20.refs_1_.q_ref, bf16[4096,128]{1,0:T(8,128)(2,1)S(1)} %copy-done.3, bf16[128,4096]{1,0:T(8,128)(2,1)S(1)} %copy-done.5, bf16[128,4096]{1,0:T(8,128)(2,1)S(1)} %copy-done.7, ...), custom_call_target="tpu_custom_call" | custom-call | flops 2684354560 | bytes 1048576 | tf_op jit(solution)/shard_map/piece/pallas_call | solution.py:221
  32.7 0.0 collective-permute-done.1.refs_7_
  32.7 5.8 %piece.4 = (f32[4096,128]{1,0:T(8,128)S(1)}, bf16[512,256]{1,0:T(8,128)(2,1)S(1)}) custom-call(s32[1]{0:T(128)} %bitcast.7.refs_0_, bf16[4096,128]{1,0:T(8,128)(2,1)S(1)} %get-tuple-element.20.refs_1_.q_ref, bf16[4096,128]{1,0:T(8,128)(2,1)S(1)} %copy-done.3, bf16[128,4096]{1,0:T(8,128)(2,1)S(1)} %copy-done.5, ...), custom_call_target="tpu_custom_call", output_to_operand_aliasing={{0}: (8, {})} | custom-call | flops 2684354560 | bytes 1048576 | tf_op jit(solution)/shard_map/piece/pallas_call | solution.py:221
  38.5 0.0 collective-permute-done.refs_7_
  38.6 0.0 copy-start.8
  38.6 4.9 %piece.5 = (f32[4096,128]{1,0:T(8,128)S(1)}, bf16[512,256]{1,0:T(8,128)(2,1)S(1)}) custom-call(s32[1]{0:T(128)} %bitcast.7.refs_0_, bf16[4096,128]{1,0:T(8,128)(2,1)S(1)} %get-tuple-element.20.refs_1_.q_ref, bf16[4096,128]{1,0:T(8,128)(2,1)S(1)} %copy-done.3, bf16[128,4096]{1,0:T(8,128)(2,1)S(1)} %copy-done.5, ...), custom_call_target="tpu_custom_call", output_to_operand_aliasing={{0}: (8, {})} | custom-call | flops 2684354560 | bytes 1048576 | tf_op jit(solution)/shard_map/piece/pallas_call | solution.py:221
  43.4 0.1 collective-permute-start.5
  43.5 3.5 %collective-permute-start.4 = (bf16[512,256]{1,0:T(8,128)(2,1)S(1)}, bf16[512,256]{1,0:T(8,128)(2,1)S(1)}, u32[]{:S(2)}, u32[]{:S(2)}) collective-permute-start(bf16[512,256]{1,0:T(8,128)(2,1)S(1)} %get-tuple-element.35), channel_id=1, source_target_pairs={{0,128},{4,132},{8,136},{12,140},{16,144},{20,148},{24,152},{28,15... | collective-permute-start | bytes 786440 | tf_op jit(solution)/shard_map/ppermute | solution.py:280
  47.1 0.1 collective-permute-start.3
  47.2 0.0 copy-done.8
  47.2 0.0 copy-start.10
  47.2 4.6 %own.1 = (bf16[512,1024]{1,0:T(8,128)(2,1)}, bf16[512,256]{1,0:T(8,128)(2,1)}) custom-call(bf16[4096,128]{1,0:T(8,128)(2,1)S(1)} %get-tuple-element.20.refs_1_.q_ref, bf16[4096,128]{1,0:T(8,128)(2,1)S(1)} %copy-done.3, bf16[128,4096]{1,0:T(8,128)(2,1)S(1)} %copy-done.5, bf16[128,4096]{1,0:T(8,128)(2,1)S(1)} %copy-done.7, ...), custom_call_target="tpu_custom_call" | custom-call | flops 2013265920 | bytes 1048576 | tf_op jit(solution)/shard_map/own/pallas_call | solution.py:166
  51.8 2.4 %collective-permute-done.5.refs_2_ = bf16[512,256]{1,0:T(8,128)(2,1)S(1)} collective-permute-done((bf16[512,256]{1,0:T(8,128)(2,1)S(1)}, bf16[512,256]{1,0:T(8,128)(2,1)S(1)}, u32[]{:S(2)}, u32[]{:S(2)}) %collective-permute-start.5) | collective-permute-done | bytes 262176 | tf_op jit(solution)/shard_map/ppermute | solution.py:280
  54.2 5.6 %collective-permute-done.4.refs_1_ = bf16[512,256]{1,0:T(8,128)(2,1)S(1)} collective-permute-done((bf16[512,256]{1,0:T(8,128)(2,1)S(1)}, bf16[512,256]{1,0:T(8,128)(2,1)S(1)}, u32[]{:S(2)}, u32[]{:S(2)}) %collective-permute-start.4) | collective-permute-done | bytes 262176 | tf_op jit(solution)/shard_map/ppermute | solution.py:280
  59.8 3.6 %collective-permute-done.3.refs_0_ = bf16[512,256]{1,0:T(8,128)(2,1)S(1)} collective-permute-done((bf16[512,256]{1,0:T(8,128)(2,1)S(1)}, bf16[512,256]{1,0:T(8,128)(2,1)S(1)}, u32[]{:S(2)}, u32[]{:S(2)}) %collective-permute-start.3) | collective-permute-done | bytes 262176 | tf_op jit(solution)/shard_map/ppermute | solution.py:280
  63.5 0.0 copy-done.10
  63.5 1.4 %place.1 = bf16[1536,256]{1,0:T(8,128)(2,1)} custom-call(s32[3]{0:T(128)S(1)} %bitcast.17, bf16[512,256]{1,0:T(8,128)(2,1)S(1)} %collective-permute-done.3.refs_0_, bf16[512,256]{1,0:T(8,128)(2,1)S(1)} %collective-permute-done.4.refs_1_, bf16[512,256]{1,0:T(8,128)(2,1)S(1)} %collective-permute-done.5.refs_2_), custom_call_target="tpu_custom_call" | custom-call | tf_op jit(solution)/shard_map/place/pallas_call | solution.py:247
Async XLA Ops:
  0.6 0.7 %copy-start.9 = (s32[1,3]{1,0:T(1,128)S(1)}, s32[1,3]{1,0:T(1,128)}, u32[]{:S(2)}) copy-start(s32[1,3]{1,0:T(1,128)} %param.13) | copy-start | bytes 40
  3.9 17.9 %collective-permute-start.2 = (bf16[512,256]{1,0:T(8,128)(2,1)}, bf16[512,256]{1,0:T(8,128)(2,1)}, u32[]{:S(2)}, u32[]{:S(2)}) collective-permute-start(bf16[512,256]{1,0:T(8,128)(2,1)} %get-tuple-element.28), channel_id=1, source_target_pairs={{0,128},{4,132},{8,136},{12,140},{16,144},{20,148},{24,152},{28,15... | collective-permute-start | bytes 786440 | tf_op jit(solution)/shard_map/ppermute | solution.py:274
  7.0 25.7 %collective-permute-start.1 = (bf16[512,256]{1,0:T(8,128)(2,1)}, bf16[512,256]{1,0:T(8,128)(2,1)}, u32[]{:S(2)}, u32[]{:S(2)}) collective-permute-start(bf16[512,256]{1,0:T(8,128)(2,1)} %get-tuple-element.27), channel_id=1, source_target_pairs={{128,0},{132,4},{136,8},{140,12},{144,16},{148,20},{152,24},{156,2... | collective-permute-start | bytes 786440 | tf_op jit(solution)/shard_map/ppermute | solution.py:274
  8.3 30.3 %collective-permute-start = (bf16[512,256]{1,0:T(8,128)(2,1)}, bf16[512,256]{1,0:T(8,128)(2,1)S(1)}, u32[]{:S(2)}, u32[]{:S(2)}) collective-permute-start(bf16[512,256]{1,0:T(8,128)(2,1)} %get-tuple-element.26), channel_id=1, source_target_pairs={{0,128},{4,132},{8,136},{12,140},{16,144},{20,148},{24,152},{28,15... | collective-permute-start | bytes 786440 | tf_op jit(solution)/shard_map/ppermute | solution.py:274
  17.5 1.3 %copy-start = (f32[4096,128]{1,0:T(8,128)}, f32[4096,128]{1,0:T(8,128)S(1)}, u32[]{:S(2)}) copy-start(f32[4096,128]{1,0:T(8,128)S(1)} %get-tuple-element.25.refs_6_.o_ref) | copy-start | bytes 6291460
  18.9 1.0 %copy-start.2 = (bf16[4096,128]{1,0:T(8,128)(2,1)}, bf16[4096,128]{1,0:T(8,128)(2,1)S(1)}, u32[]{:S(2)}) copy-start(bf16[4096,128]{1,0:T(8,128)(2,1)S(1)} %get-tuple-element.21.refs_2_.do_ref) | copy-start | bytes 3145732
  19.8 1.0 %copy-start.4 = (bf16[128,4096]{1,0:T(8,128)(2,1)}, bf16[128,4096]{1,0:T(8,128)(2,1)S(1)}, u32[]{:S(2)}) copy-start(bf16[128,4096]{1,0:T(8,128)(2,1)S(1)} %get-tuple-element.22.refs_3_.qt_ref) | copy-start | bytes 3145732
  20.8 1.0 %copy-start.6 = (bf16[128,4096]{1,0:T(8,128)(2,1)}, bf16[128,4096]{1,0:T(8,128)(2,1)S(1)}, u32[]{:S(2)}) copy-start(bf16[128,4096]{1,0:T(8,128)(2,1)S(1)} %get-tuple-element.23.refs_4_.dot_ref) | copy-start | bytes 3145732
  21.8 1.6 %copy-start.1 = (f32[4096,128]{1,0:T(8,128)S(1)}, f32[4096,128]{1,0:T(8,128)}, u32[]{:S(2)}) copy-start(f32[4096,128]{1,0:T(8,128)} %copy-done) | copy-start | bytes 6291460
  23.4 1.2 %copy-start.3 = (bf16[4096,128]{1,0:T(8,128)(2,1)S(1)}, bf16[4096,128]{1,0:T(8,128)(2,1)}, u32[]{:S(2)}) copy-start(bf16[4096,128]{1,0:T(8,128)(2,1)} %copy-done.2) | copy-start | bytes 3145732
  24.6 1.2 %copy-start.5 = (bf16[128,4096]{1,0:T(8,128)(2,1)S(1)}, bf16[128,4096]{1,0:T(8,128)(2,1)}, u32[]{:S(2)}) copy-start(bf16[128,4096]{1,0:T(8,128)(2,1)} %copy-done.4) | copy-start | bytes 3145732
  25.8 1.2 %copy-start.7 = (bf16[128,4096]{1,0:T(8,128)(2,1)S(1)}, bf16[128,4096]{1,0:T(8,128)(2,1)}, u32[]{:S(2)}) copy-start(bf16[128,4096]{1,0:T(8,128)(2,1)} %copy-done.6) | copy-start | bytes 3145732
  38.6 8.6 %copy-start.8 = (bf16[1,512,256]{2,1,0:T(8,128)(2,1)S(1)}, bf16[1,512,256]{2,1,0:T(8,128)(2,1)}, u32[]{:S(2)}) copy-start(bf16[1,512,256]{2,1,0:T(8,128)(2,1)} %param.11) | copy-start | bytes 786436
  43.4 10.8 %collective-permute-start.5 = (bf16[512,256]{1,0:T(8,128)(2,1)S(1)}, bf16[512,256]{1,0:T(8,128)(2,1)S(1)}, u32[]{:S(2)}, u32[]{:S(2)}) collective-permute-start(bf16[512,256]{1,0:T(8,128)(2,1)S(1)} %get-tuple-element.36), channel_id=1, source_target_pairs={{0,128},{4,132},{8,136},{12,140},{16,144},{20,148},{24,152},{28,15... | collective-permute-start | bytes 786440 | tf_op jit(solution)/shard_map/ppermute | solution.py:280
  43.5 16.3 %collective-permute-start.4 = (bf16[512,256]{1,0:T(8,128)(2,1)S(1)}, bf16[512,256]{1,0:T(8,128)(2,1)S(1)}, u32[]{:S(2)}, u32[]{:S(2)}) collective-permute-start(bf16[512,256]{1,0:T(8,128)(2,1)S(1)} %get-tuple-element.35), channel_id=1, source_target_pairs={{0,128},{4,132},{8,136},{12,140},{16,144},{20,148},{24,152},{28,15... | collective-permute-start | bytes 786440 | tf_op jit(solution)/shard_map/ppermute | solution.py:280
  47.1 16.4 %collective-permute-start.3 = (bf16[512,256]{1,0:T(8,128)(2,1)S(1)}, bf16[512,256]{1,0:T(8,128)(2,1)S(1)}, u32[]{:S(2)}, u32[]{:S(2)}) collective-permute-start(bf16[512,256]{1,0:T(8,128)(2,1)S(1)} %get-tuple-element.34), channel_id=1, source_target_pairs={{0,128},{4,132},{8,136},{12,140},{16,144},{20,148},{24,152},{28,15... | collective-permute-start | bytes 786440 | tf_op jit(solution)/shard_map/ppermute | solution.py:280
  47.2 16.3 %copy-start.10 = (s32[1,3]{1,0:T(1,128)S(1)}, s32[1,3]{1,0:T(1,128)}, u32[]{:S(2)}) copy-start(s32[1,3]{1,0:T(1,128)} %param.13) | copy-start | bytes 40

commit v3 on v2

v3 whole, which is shorter than its diff:
```python
import functools

import jax
import jax.numpy as jnp
from jax import lax
from jax.experimental import pallas as pl
from jax.experimental.pallas import tpu as pltpu
from jax.sharding import PartitionSpec as P


NSL = 4
LOG2E = 1.4426950408889634
F32 = jnp.float32
BF16 = jnp.bfloat16
VMEM = pl.BlockSpec(memory_space=pltpu.VMEM)
SMEM = pl.BlockSpec(memory_space=pltpu.SMEM)
HBM = pl.BlockSpec(memory_space=pltpu.HBM)
BLOCKS = (0, 2, 1)
PIECES = ((0, 0, 512), (2, 0, 512), (1, 0, 256), (1, 256, 256))


def dot(a, b, ca, cb):
    return lax.dot_general(a, b, (((ca,), (cb,)), ((), ())), preferred_element_type=F32)


def in_hbm(x):
    return pltpu.with_memory_space_constraint(x, pltpu.HBM)


def params(mib):
    return pltpu.CompilerParams(vmem_limit_bytes=mib << 20)


def cost(rows, keys, heads, dh):
    return pl.CostEstimate(
        flops=10 * rows * keys * heads * dh, bytes_accessed=1 << 20, transcendentals=rows * keys * heads
    )


def pick_kernel(rows, table_hbm, pool_ref, *refs):
    outs, table_ref, sem = refs[:-2], refs[-2], refs[-1]
    first = pltpu.make_async_copy(table_hbm, table_ref, sem.at[len(BLOCKS)])
    first.start()
    first.wait()
    copies = []
    for i, block in enumerate(BLOCKS):
        at = pl.multiple_of(table_ref[0, block] * rows, 128)
        copies.append(pltpu.make_async_copy(pool_ref.at[pl.ds(at, rows), :], outs[i], sem.at[i]))
    for c in copies:
        c.start()
    for c in copies:
        c.wait()


def pick(table, pool, rows):
    width = pool.shape[1]
    return pl.pallas_call(
        functools.partial(pick_kernel, rows),
        in_specs=[HBM, HBM],
        out_specs=[VMEM] * len(BLOCKS),
        out_shape=[jax.ShapeDtypeStruct((rows, width), pool.dtype)] * len(BLOCKS),
        scratch_shapes=[pltpu.SMEM(table.shape, jnp.int32), pltpu.SemaphoreType.DMA((len(BLOCKS) + 1,))],
        compiler_params=params(4),
        name="pick",
    )(in_hbm(table), in_hbm(pool))


def stretch(ref, c, heads):
    half, dh = ref.shape[0] // 2, ref.shape[1] // heads
    t, h0 = c // 2, (c % 2) * (heads // 2)
    rs = slice(t * half, (t + 1) * half)
    return jnp.concatenate([ref[rs, h * dh : (h + 1) * dh] for h in range(h0, h0 + heads // 2)], axis=0)


def prep_kernel(heads, dh, q_hbm, do_hbm, l_hbm, o_hbm, q_ref, do_ref, qt_ref, dot_ref, l_ref, o_ref, lraw_ref, oraw_ref, sem):
    rows = lraw_ref.shape[1]
    half = rows // 2
    small = [pltpu.make_async_copy(l_hbm, lraw_ref, sem.at[0]), pltpu.make_async_copy(o_hbm, oraw_ref, sem.at[1])]
    large = []
    for t in range(2):
        for a, b in ((q_hbm, q_ref), (do_hbm, do_ref)):
            rs = pl.ds(t * half, half)
            large.append(pltpu.make_async_copy(a.at[rs, :], b.at[rs, :], sem.at[2 + len(large)]))
    for c in small + large:
        c.start()
    for c in small:
        c.wait()
    lcol = (lraw_ref[...].astype(F32) * LOG2E).T
    ocol = oraw_ref[...].astype(F32).T
    for t in range(2):
        rs = slice(t * half, (t + 1) * half)
        for h in range(heads):
            part = slice((t * heads + h) * half, (t * heads + h + 1) * half)
            l_ref[part, :] = jnp.broadcast_to(lcol[rs, h : h + 1], (half, dh))
            o_ref[part, :] = jnp.broadcast_to(ocol[rs, h : h + 1], (half, dh))
    for t in range(2):
        rs = slice(t * half, (t + 1) * half)
        for i, (a, b) in enumerate(((q_ref, qt_ref), (do_ref, dot_ref))):
            large[2 * t + i].wait()
            for h in range(heads):
                part = slice((t * heads + h) * half, (t * heads + h + 1) * half)
                b[:, part] = a[rs, h * dh : (h + 1) * dh].T


def prep(q, do, totals, offsets):
    rows, width = q.shape
    heads = totals.shape[0]
    dh = width // heads
    many = heads * rows
    return pl.pallas_call(
        functools.partial(prep_kernel, heads, dh),
        in_specs=[HBM] * 4,
        out_specs=[VMEM] * 6,
        out_shape=[
            jax.ShapeDtypeStruct((rows, width), BF16),
            jax.ShapeDtypeStruct((rows, width), BF16),
            jax.ShapeDtypeStruct((dh, many), BF16),
            jax.ShapeDtypeStruct((dh, many), BF16),
            jax.ShapeDtypeStruct((many, dh), F32),
            jax.ShapeDtypeStruct((many, dh), F32),
        ],
        scratch_shapes=[
            pltpu.VMEM((heads, rows), BF16),
            pltpu.VMEM((heads, rows), BF16),
            pltpu.SemaphoreType.DMA((6,)),
        ],
        compiler_params=params(16),
        cost_estimate=pl.CostEstimate(flops=1000, bytes_accessed=4 << 20, transcendentals=0),
        name="prep",
    )(*(in_hbm(x) for x in (q, do, totals, offsets)))


def own_kernel(heads, scale, q_ref, do_ref, qt_ref, dot_ref, l_ref, o_ref, kv_ref, pool_ref, out_hbm, g_hbm, out_ref, g_ref, dk_ref, dv_ref, sem):
    many, dh = l_ref.shape
    half = many // heads // 2
    step = many // 4
    key_ids = lax.broadcasted_iota(jnp.int32, (step, half), 1)
    row_ids = lax.rem(lax.broadcasted_iota(jnp.int32, (step, half), 0), half)
    visible = key_ids <= row_ids
    k, v = kv_ref[:, :dh], kv_ref[:, dh:]
    copies = []
    for c in (2, 3, 0, 1):
        t = c // 2
        rs = slice(c * step, (c + 1) * step)
        keys = (t + 1) * half
        over = keys // dh
        s = dot(stretch(q_ref, c, heads), k[:keys], 1, 1)
        dp = dot(stretch(do_ref, c, heads), v[:keys], 1, 1)
        p = jnp.exp2(s * (scale * LOG2E) - jnp.concatenate([l_ref[rs, :]] * over, axis=1))
        last = jnp.where(visible, p[:, keys - half :], 0.0)
        p = last if t == 0 else jnp.concatenate([p[:, :half], last], axis=1)
        ds = (p * (dp - jnp.concatenate([o_ref[rs, :]] * over, axis=1))).astype(BF16)
        dq = dot(ds, k[:keys], 1, 0)
        for i in range(heads // 2):
            h = (c % 2) * (heads // 2) + i
            pool_term = (pool_ref[c * step + i * half : c * step + (i + 1) * half, :] * scale).astype(BF16).astype(F32)
            total = dq[i * half : (i + 1) * half, :] * scale + pool_term
            out_ref[t * half : (t + 1) * half, h * dh : (h + 1) * dh] = total.astype(BF16)
        wide = heads // 2 * dh
        place_of = (pl.ds(t * half, half), pl.ds(c % 2 * wide, wide))
        copies.append(pltpu.make_async_copy(out_ref.at[place_of], out_hbm.at[place_of], sem.at[c]))
        copies[-1].start()
        dk = dot(qt_ref[:, rs], ds, 1, 0)
        dv = dot(dot_ref[:, rs], p.astype(BF16), 1, 0)
        if c == 2:
            dk_ref[...] = dk
            dv_ref[...] = dv
        else:
            dk_ref[:, :keys] += dk
            dv_ref[:, :keys] += dv
    g_ref[:, :dh] = (dk_ref[...].T * scale).astype(BF16)
    g_ref[:, dh:] = dv_ref[...].T.astype(BF16)
    copies.append(pltpu.make_async_copy(g_ref, g_hbm, sem.at[4]))
    copies[-1].start()
    for copy in copies:
        copy.wait()


def own(rows_of, kv, pool_dq):
    many, dh = pool_dq.shape
    rows = kv.shape[0]
    heads = many // rows
    return pl.pallas_call(
        functools.partial(own_kernel, heads, dh**-0.5),
        in_specs=[VMEM] * 8,
        out_specs=[HBM] * 2,
        out_shape=[jax.ShapeDtypeStruct((rows, heads * dh), BF16), jax.ShapeDtypeStruct((rows, 2 * dh), BF16)],
        scratch_shapes=[
            pltpu.VMEM((rows, heads * dh), BF16),
            pltpu.VMEM((rows, 2 * dh), BF16),
            pltpu.VMEM((dh, rows), F32),
            pltpu.VMEM((dh, rows), F32),
            pltpu.SemaphoreType.DMA((5,)),
        ],
        compiler_params=params(24),
        cost_estimate=cost(many, rows * 3 // 4, 1, dh),
        name="own",
    )(*rows_of, kv, pool_dq)


def piece_kernel(heads, scale, block, start, first, *refs):
    depth_ref, q_ref, do_ref, qt_ref, dot_ref, l_ref, o_ref, kv_ref = refs[:8]
    split = block == 1
    from_ref = None if first else refs[8]
    outs = refs[8 + (not first) + (split and start > 0) :]
    dq_ref, g_ref = outs[:2]
    next_ref = outs[2] if split and start == 0 else None
    dk_ref, dv_ref = outs[-2:]
    many, dh = l_ref.shape
    step = many // 4
    size = g_ref.shape[0]

    def work(keys, to):
        k, v = kv_ref[start : start + keys, :dh], kv_ref[start : start + keys, dh:]
        over = keys // dh
        for c in range(4):
            rs = slice(c * step, (c + 1) * step)
            s = dot(stretch(q_ref, c, heads), k, 1, 1)
            dp = dot(stretch(do_ref, c, heads), v, 1, 1)
            p = jnp.exp2(s * (scale * LOG2E) - jnp.concatenate([l_ref[rs, :]] * over, axis=1))
            ds = (p * (dp - jnp.concatenate([o_ref[rs, :]] * over, axis=1))).astype(BF16)
            part = dot(ds, k, 1, 0)
            dq_ref[rs, :] = part if first else from_ref[rs, :] + part
            dk = dot(qt_ref[:, rs], ds, 1, 0)
            dv = dot(dot_ref[:, rs], p.astype(BF16), 1, 0)
            if c == 0:
                dk_ref[:, :keys] = dk
                dv_ref[:, :keys] = dv
            else:
                dk_ref[:, :keys] += dk
                dv_ref[:, :keys] += dv
        for i, ref in enumerate(to):
            ks = slice(i * size, (i + 1) * size)
            ref[:, :dh] = (dk_ref[:, ks].T * scale).astype(BF16)
            ref[:, dh:] = dv_ref[:, ks].T.astype(BF16)

    if block == 0:
        work(size, (g_ref,))
        return

    @pl.when(depth_ref[0] == NSL - 1)
    def _():
        work(size, (g_ref,))

    if split and start > 0:
        return
    unused = depth_ref[0] <= block
    if split:

        @pl.when(depth_ref[0] == NSL - 2)
        def _():
            work(2 * size, (g_ref, next_ref))

    @pl.when(unused)
    def _():
        g_ref[...] = jnp.zeros_like(g_ref)
        if split:
            next_ref[...] = jnp.zeros_like(next_ref)


def piece(depth, rows_of, kv, dq, held, block, start, size):
    many, dh = rows_of[-1].shape
    split = block == 1
    args = (depth, *rows_of, kv) + (() if dq is None else (dq,)) + (() if held is None else (held,))
    gave = jax.ShapeDtypeStruct((size, 2 * dh), BF16)
    keys = 2 * size if split and start == 0 else size
    return pl.pallas_call(
        functools.partial(piece_kernel, many // kv.shape[0], dh**-0.5, block, start, dq is None),
        in_specs=[SMEM] + [VMEM] * (len(args) - 1),
        out_specs=[VMEM] * (3 if split and start == 0 else 2),
        out_shape=[jax.ShapeDtypeStruct((many, dh), F32), gave] + ([gave] if split and start == 0 else []),
        scratch_shapes=[pltpu.VMEM((dh, keys), F32), pltpu.VMEM((dh, keys), F32)],
        input_output_aliases=({} if dq is None else {8: 0}) | ({} if held is None else {9: 1}),
        compiler_params=params(24),
        cost_estimate=cost(many, size, 1, dh),
        name="piece",
    )(*args)


def place_kernel(rows, table_ref, *refs):
    ins, out_ref, sem = refs[: len(PIECES)], refs[-2], refs[-1]
    copies = []
    for i, (block, first, size) in enumerate(PIECES):
        at = pl.multiple_of(table_ref[block] * rows + first, 128)
        copies.append(pltpu.make_async_copy(ins[i], out_ref.at[pl.ds(at, size), :], sem.at[i]))
    for c in copies:
        c.start()
    for c in copies:
        c.wait()


def place(table, parts, shape, rows):
    return pl.pallas_call(
        functools.partial(place_kernel, rows),
        in_specs=[SMEM] + [VMEM] * len(parts),
        out_specs=HBM,
        out_shape=jax.ShapeDtypeStruct(shape, BF16),
        scratch_shapes=[pltpu.SemaphoreType.DMA((len(PIECES),))],
        compiler_params=params(4),
        name="place",
    )(table, *parts)


def per_device(query, grad_output, log_total, offset, slice_keys, pool_keys, block_table):
    rows, _ = log_total.shape[1:]
    table = block_table[0]
    sections = lax.axis_size("section")
    half_axis = sections // 2
    group = sections // NSL
    depths = [NSL - 1 - layer // group % (NSL - 1) for layer in range(sections)]
    me = lax.axis_index("section")
    depth = (NSL - 1 - me // group % (NSL - 1)).astype(jnp.int32).reshape(1)

    swap = [(layer, (layer + half_axis) % sections) for layer in range(sections)]
    home = [(layer, p) for layer, p in swap if depths[layer] == NSL - 1]
    deep = [(p, layer) for layer, p in swap if depths[layer] == NSL - 1]

    picked = pick(block_table, pool_keys[0], rows)
    arrived = {}
    for i, block in enumerate(BLOCKS):
        arrived[block] = lax.ppermute(picked[i], "section", deep if block == NSL - 2 else swap)
    rows_of = prep(query[0], grad_output[0], log_total[0].T, offset[0].T)
    dq = held = None
    parts = []
    for block, start, size in PIECES:
        dq, g, *rest = piece(depth, rows_of, arrived[block], dq, held, block, start, size)
        held = rest[0] if rest else None
        parts.append(lax.ppermute(g, "section", home if block == NSL - 2 else swap))
    query_grad, slice_grad = own(rows_of, slice_keys[0], dq)
    pool_grad = place(table, parts, pool_keys.shape[1:], rows)
    return (query_grad[None], slice_grad[None], pool_grad[None])


def solution(mesh):
    spec = P("section", None, "kv")
    return jax.shard_map(
        per_device,
        mesh=mesh,
        in_specs=(spec, spec, spec, spec, spec, spec, P("section", None)),
        out_specs=(spec, spec, spec),
        check_vma=False,
    )
```

time: 65.5 us -> 56.8 us (0.87)
  the two profiles are of different devices: /device:TPU:8 before, /device:TPU:28 now
where the time goes in v3:
time: 56.8 us; the launch traced here: 56.4 us
  starting transfers between devices  21.5 us (38%)
  Pallas kernels  18.1 us (32%)
  local copies, waits for them, and re-layouts  9.5 us (17%)
  waiting for transfers between devices  6.3 us (11%)
  between operations  0.91 us (2%)
    ppermute x4, starting transfers between devices, per_device(): parts.append(lax.ppermute(g, 'section', home if block == NSL - 2 else swap))  15.3 us
    unnamed x20, local copies, waits for them, and re-layouts  9.5 us
    pallas_call x4, Pallas kernels, piece(): pl.pallas_call(functools.partial(piece_kernel, many // kv.shape[0], dh **...  6.9 us
    ppermute x4, waiting for transfers between devices, per_device(): parts.append(lax.ppermute(g, 'section', home if block == NSL - 2 else swap))  6.29 us
    ppermute x3, starting transfers between devices, per_device(): lax.ppermute(picked[i], 'section', deep if block == NSL - 2 else swap)  6.24 us
    pallas_call x1, Pallas kernels, own(): pl.pallas_call(functools.partial(own_kernel, heads, dh ** (-0.5)), in_spe...  4.49 us
    pallas_call x1, Pallas kernels, pick(): pl.pallas_call(functools.partial(pick_kernel, rows), in_specs=[HBM, HBM],...  2.69 us
    pallas_call x1, Pallas kernels, prep(): pl.pallas_call(functools.partial(prep_kernel, heads, dh), in_specs=[HBM]...  2.6 us
  transfers between devices with their start and end apart: 7, of which 2 were waited for; matrix products, arithmetic and copies ran while one was open for 0% of the time, Pallas kernels for 25%

profile of v3, /device:TPU:28, one launch (start us, length us, event | category | flops | bytes accessed | tf_op | source)
XLA Modules:
  0.0 56.4 jit_solution(16367807074777535990)
XLA Ops:
  0.6 2.7 %pick.1 = (bf16[512,256]{1,0:T(8,128)(2,1)}, bf16[512,256]{1,0:T(8,128)(2,1)}, bf16[512,256]{1,0:T(8,128)(2,1)}) custom-call(s32[1,3]{1,0:T(1,128)} %table_hbm.1, bf16[1536,256]{1,0:T(8,128)(2,1)} %bitcast.20), custom_call_target="tpu_custom_call" | custom-call | tf_op jit(solution)/shard_map/pick/pallas_call | solution.py:57
  3.3 0.6 %collective-permute-start.2 = (bf16[512,256]{1,0:T(8,128)(2,1)}, bf16[512,256]{1,0:T(8,128)(2,1)}, u32[]{:S(2)}, u32[]{:S(2)}) collective-permute-start(bf16[512,256]{1,0:T(8,128)(2,1)} %get-tuple-element.31), channel_id=1, source_target_pairs={{0,128},{4,132},{8,136},{12,140},{16,144},{20,148},{24,152},{28,15... | collective-permute-start | bytes 786440 | tf_op jit(solution)/shard_map/ppermute | solution.py:321
  3.9 5.6 %collective-permute-start.1 = (bf16[512,256]{1,0:T(8,128)(2,1)}, bf16[512,256]{1,0:T(8,128)(2,1)}, u32[]{:S(2)}, u32[]{:S(2)}) collective-permute-start(bf16[512,256]{1,0:T(8,128)(2,1)} %get-tuple-element.30), channel_id=1, source_target_pairs={{128,0},{132,4},{136,8},{140,12},{144,16},{148,20},{152,24},{156,2... | collective-permute-start | bytes 786440 | tf_op jit(solution)/shard_map/ppermute | solution.py:321
  9.6 0.0 collective-permute-start
  9.6 2.6 %prep.1 = (bf16[512,1024]{1,0:T(8,128)(2,1)S(1)}, bf16[512,1024]{1,0:T(8,128)(2,1)S(1)}, bf16[128,4096]{1,0:T(8,128)(2,1)S(1)}, bf16[128,4096]{1,0:T(8,128)(2,1)...) custom-call(bf16[512,1024]{1,0:T(8,128)(2,1)} %bitcast.17, bf16[512,1024]{1,0:T(8,128)(2,1)} %bitcast.18, ...), custom_call_target="tpu_custom_call" | custom-call | flops 1000 | bytes 4194304 | tf_op jit(solution)/shard_map/prep/pallas_call | solution.py:110
  12.2 0.0 copy-start
  12.2 1.3 %copy-done = f32[4096,128]{1,0:T(8,128)} copy-done((f32[4096,128]{1,0:T(8,128)}, f32[4096,128]{1,0:T(8,128)S(1)}, u32[]{:S(2)}) %copy-start) | copy-done | bytes 2097176
  13.5 0.0 copy-start.2
  13.5 1.0 %copy-done.2 = bf16[512,1024]{1,0:T(8,128)(2,1)} copy-done((bf16[512,1024]{1,0:T(8,128)(2,1)}, bf16[512,1024]{1,0:T(8,128)(2,1)S(1)}, u32[]{:S(2)}) %copy-start.2) | copy-done | bytes 1048600
  14.5 0.0 copy-start.4
  14.5 1.0 %copy-done.4 = bf16[128,4096]{1,0:T(8,128)(2,1)} copy-done((bf16[128,4096]{1,0:T(8,128)(2,1)}, bf16[128,4096]{1,0:T(8,128)(2,1)S(1)}, u32[]{:S(2)}) %copy-start.4) | copy-done | bytes 1048600
  15.5 0.0 copy-start.6
  15.5 1.0 %copy-done.6 = bf16[128,4096]{1,0:T(8,128)(2,1)} copy-done((bf16[128,4096]{1,0:T(8,128)(2,1)}, bf16[128,4096]{1,0:T(8,128)(2,1)S(1)}, u32[]{:S(2)}) %copy-start.6) | copy-done | bytes 1048600
  16.4 0.0 collective-permute-done.2.refs_7_
  16.4 0.0 copy-start.1
  16.4 1.6 %copy-done.1 = f32[4096,128]{1,0:T(8,128)S(1)} copy-done((f32[4096,128]{1,0:T(8,128)S(1)}, f32[4096,128]{1,0:T(8,128)}, u32[]{:S(2)}) %copy-start.1) | copy-done | bytes 2097176
  18.0 0.0 copy-start.3
  18.0 1.2 %copy-done.3 = bf16[512,1024]{1,0:T(8,128)(2,1)S(1)} copy-done((bf16[512,1024]{1,0:T(8,128)(2,1)S(1)}, bf16[512,1024]{1,0:T(8,128)(2,1)}, u32[]{:S(2)}) %copy-start.3) | copy-done | bytes 1048600
  19.2 0.0 copy-start.5
  19.2 1.2 %copy-done.5 = bf16[128,4096]{1,0:T(8,128)(2,1)S(1)} copy-done((bf16[128,4096]{1,0:T(8,128)(2,1)S(1)}, bf16[128,4096]{1,0:T(8,128)(2,1)}, u32[]{:S(2)}) %copy-start.5) | copy-done | bytes 1048600
  20.5 0.0 copy-start.7
  20.5 1.2 %copy-done.7 = bf16[128,4096]{1,0:T(8,128)(2,1)S(1)} copy-done((bf16[128,4096]{1,0:T(8,128)(2,1)S(1)}, bf16[128,4096]{1,0:T(8,128)(2,1)}, u32[]{:S(2)}) %copy-start.7) | copy-done | bytes 1048600
  21.7 5.7 %piece.4 = (f32[4096,128]{1,0:T(8,128)S(1)}, bf16[512,256]{1,0:T(8,128)(2,1)S(1)}) custom-call(s32[1]{0:T(128)} %bitcast.7.refs_0_, bf16[512,1024]{1,0:T(8,128)(2,1)S(1)} %get-tuple-element.23.refs_1_.q_ref, bf16[512,1024]{1,0:T(8,128)(2,1)S(1)} %copy-done.3, bf16[128,4096]{1,0:T(8,128)(2,1)S(1)} %copy-done.5, bf16[128,4096]{1,0:T(8,128)(2,1)S(1)} %copy-done.7, ...), custom_call_target="tpu_custom_call" | custom-call | flops 2684354560 | bytes 1048576 | tf_op jit(solution)/shard_map/piece/pallas_call | solution.py:267
  27.4 0.0 collective-permute-done.1.refs_7_
  27.4 1.0 %piece.5 = (f32[4096,128]{1,0:T(8,128)S(1)}, bf16[512,256]{1,0:T(8,128)(2,1)S(1)}) custom-call(s32[1]{0:T(128)} %bitcast.7.refs_0_, bf16[512,1024]{1,0:T(8,128)(2,1)S(1)} %get-tuple-element.23.refs_1_.q_ref, bf16[512,1024]{1,0:T(8,128)(2,1)S(1)} %copy-done.3, bf16[128,4096]{1,0:T(8,128)(2,1)S(1)} %copy-done.5, ...), custom_call_target="tpu_custom_call", output_to_operand_aliasing={{0}: (8, {})} | custom-call | flops 2684354560 | bytes 1048576 | tf_op jit(solution)/shard_map/piece/pallas_call | solution.py:267
  28.4 1.3 %collective-permute-start.4 = (bf16[512,256]{1,0:T(8,128)(2,1)S(1)}, bf16[512,256]{1,0:T(8,128)(2,1)S(1)}, u32[]{:S(2)}, u32[]{:S(2)}) collective-permute-start(bf16[512,256]{1,0:T(8,128)(2,1)S(1)} %get-tuple-element.40), channel_id=1, source_target_pairs={{0,128},{4,132},{8,136},{12,140},{16,144},{20,148},{24,152},{28,15... | collective-permute-start | bytes 786440 | tf_op jit(solution)/shard_map/ppermute | solution.py:328
  29.7 8.5 %collective-permute-start.3 = (bf16[512,256]{1,0:T(8,128)(2,1)S(1)}, bf16[512,256]{1,0:T(8,128)(2,1)S(1)}, u32[]{:S(2)}, u32[]{:S(2)}) collective-permute-start(bf16[512,256]{1,0:T(8,128)(2,1)S(1)} %get-tuple-element.39), channel_id=1, source_target_pairs={{0,128},{4,132},{8,136},{12,140},{16,144},{20,148},{24,152},{28,15... | collective-permute-start | bytes 786440 | tf_op jit(solution)/shard_map/ppermute | solution.py:328
  38.2 0.0 collective-permute-done.refs_7_
  38.2 0.2 piece.6
  38.4 0.0 copy-start.8
  38.4 5.4 %collective-permute-start.6 = (bf16[256,256]{1,0:T(8,128)(2,1)S(1)}, bf16[256,256]{1,0:T(8,128)(2,1)S(1)}, u32[]{:S(2)}, u32[]{:S(2)}) collective-permute-start(bf16[256,256]{1,0:T(8,128)(2,1)S(1)} %get-tuple-element.42), channel_id=1, source_target_pairs={{0,128},{4,132},{8,136},{12,140},{16,144},{20,148},{24,152},{28,15... | collective-permute-start | bytes 393224 | tf_op jit(solution)/shard_map/ppermute | solution.py:328
  43.8 0.1 collective-permute-start.5
  43.9 0.0 copy-done.8
  43.9 0.0 copy-start.9
  43.9 4.5 %own.1 = (bf16[512,1024]{1,0:T(8,128)(2,1)}, bf16[512,256]{1,0:T(8,128)(2,1)}) custom-call(bf16[512,1024]{1,0:T(8,128)(2,1)S(1)} %get-tuple-element.23.refs_1_.q_ref, bf16[512,1024]{1,0:T(8,128)(2,1)S(1)} %copy-done.3, bf16[128,4096]{1,0:T(8,128)(2,1)S(1)} %copy-done.5, bf16[128,4096]{1,0:T(8,128)(2,1)S(1)} %copy-done.7, ...), custom_call_target="tpu_custom_call" | custom-call | flops 2013265920 | bytes 1048576 | tf_op jit(solution)/shard_map/own/pallas_call | solution.py:183
  48.4 4.9 %collective-permute-done.6.refs_3_ = bf16[256,256]{1,0:T(8,128)(2,1)S(1)} collective-permute-done((bf16[256,256]{1,0:T(8,128)(2,1)S(1)}, bf16[256,256]{1,0:T(8,128)(2,1)S(1)}, u32[]{:S(2)}, u32[]{:S(2)}) %collective-permute-start.6) | collective-permute-done | bytes 131104 | tf_op jit(solution)/shard_map/ppermute | solution.py:328
  53.3 1.4 %collective-permute-done.5.refs_2_ = bf16[256,256]{1,0:T(8,128)(2,1)S(1)} collective-permute-done((bf16[256,256]{1,0:T(8,128)(2,1)S(1)}, bf16[256,256]{1,0:T(8,128)(2,1)S(1)}, u32[]{:S(2)}, u32[]{:S(2)}) %collective-permute-start.5) | collective-permute-done | bytes 131104 | tf_op jit(solution)/shard_map/ppermute | solution.py:328
  54.7 0.0 collective-permute-done.4.refs_1_
  54.7 0.0 collective-permute-done.3.refs_0_
  54.7 0.0 copy-done.9
  54.7 1.5 %place.1 = bf16[1536,256]{1,0:T(8,128)(2,1)} custom-call(s32[3]{0:T(128)S(1)} %bitcast.16, bf16[512,256]{1,0:T(8,128)(2,1)S(1)} %collective-permute-done.3.refs_0_, bf16[512,256]{1,0:T(8,128)(2,1)S(1)} %collective-permute-done.4.refs_1_, bf16[256,256]{1,0:T(8,128)(2,1)S(1)} %collective-permute-done.5.refs_2_, bf16[256,256]{1,0:T(8,128)(2,1)S(1)} %collective-permute-done.6.refs_3_), custom_call_target="tpu_custom_call" | custom-call | tf_op jit(solution)/shard_map/place/pallas_call | solution.py:293
  (1 shorter events, 0.0 us)
Async XLA Ops:
  3.3 13.1 %collective-permute-start.2 = (bf16[512,256]{1,0:T(8,128)(2,1)}, bf16[512,256]{1,0:T(8,128)(2,1)}, u32[]{:S(2)}, u32[]{:S(2)}) collective-permute-start(bf16[512,256]{1,0:T(8,128)(2,1)} %get-tuple-element.31), channel_id=1, source_target_pairs={{0,128},{4,132},{8,136},{12,140},{16,144},{20,148},{24,152},{28,15... | collective-permute-start | bytes 786440 | tf_op jit(solution)/shard_map/ppermute | solution.py:321
  3.9 23.5 %collective-permute-start.1 = (bf16[512,256]{1,0:T(8,128)(2,1)}, bf16[512,256]{1,0:T(8,128)(2,1)}, u32[]{:S(2)}, u32[]{:S(2)}) collective-permute-start(bf16[512,256]{1,0:T(8,128)(2,1)} %get-tuple-element.30), channel_id=1, source_target_pairs={{128,0},{132,4},{136,8},{140,12},{144,16},{148,20},{152,24},{156,2... | collective-permute-start | bytes 786440 | tf_op jit(solution)/shard_map/ppermute | solution.py:321
  9.6 28.6 %collective-permute-start = (bf16[512,256]{1,0:T(8,128)(2,1)}, bf16[512,256]{1,0:T(8,128)(2,1)S(1)}, u32[]{:S(2)}, u32[]{:S(2)}) collective-permute-start(bf16[512,256]{1,0:T(8,128)(2,1)} %get-tuple-element.29), channel_id=1, source_target_pairs={{0,128},{4,132},{8,136},{12,140},{16,144},{20,148},{24,152},{28,15... | collective-permute-start | bytes 786440 | tf_op jit(solution)/shard_map/ppermute | solution.py:321
  12.2 1.3 %copy-start = (f32[4096,128]{1,0:T(8,128)}, f32[4096,128]{1,0:T(8,128)S(1)}, u32[]{:S(2)}) copy-start(f32[4096,128]{1,0:T(8,128)S(1)} %get-tuple-element.28.refs_6_.o_ref) | copy-start | bytes 6291460
  13.5 1.0 %copy-start.2 = (bf16[512,1024]{1,0:T(8,128)(2,1)}, bf16[512,1024]{1,0:T(8,128)(2,1)S(1)}, u32[]{:S(2)}) copy-start(bf16[512,1024]{1,0:T(8,128)(2,1)S(1)} %get-tuple-element.24.refs_2_.do_ref) | copy-start | bytes 3145732
  14.5 1.0 %copy-start.4 = (bf16[128,4096]{1,0:T(8,128)(2,1)}, bf16[128,4096]{1,0:T(8,128)(2,1)S(1)}, u32[]{:S(2)}) copy-start(bf16[128,4096]{1,0:T(8,128)(2,1)S(1)} %get-tuple-element.25.refs_3_.qt_ref) | copy-start | bytes 3145732
  15.5 1.0 %copy-start.6 = (bf16[128,4096]{1,0:T(8,128)(2,1)}, bf16[128,4096]{1,0:T(8,128)(2,1)S(1)}, u32[]{:S(2)}) copy-start(bf16[128,4096]{1,0:T(8,128)(2,1)S(1)} %get-tuple-element.26.refs_4_.dot_ref) | copy-start | bytes 3145732
  16.4 1.6 %copy-start.1 = (f32[4096,128]{1,0:T(8,128)S(1)}, f32[4096,128]{1,0:T(8,128)}, u32[]{:S(2)}) copy-start(f32[4096,128]{1,0:T(8,128)} %copy-done) | copy-start | bytes 6291460
  18.0 1.2 %copy-start.3 = (bf16[512,1024]{1,0:T(8,128)(2,1)S(1)}, bf16[512,1024]{1,0:T(8,128)(2,1)}, u32[]{:S(2)}) copy-start(bf16[512,1024]{1,0:T(8,128)(2,1)} %copy-done.2) | copy-start | bytes 3145732
  19.2 1.2 %copy-start.5 = (bf16[128,4096]{1,0:T(8,128)(2,1)S(1)}, bf16[128,4096]{1,0:T(8,128)(2,1)}, u32[]{:S(2)}) copy-start(bf16[128,4096]{1,0:T(8,128)(2,1)} %copy-done.4) | copy-start | bytes 3145732
  20.5 1.2 %copy-start.7 = (bf16[128,4096]{1,0:T(8,128)(2,1)S(1)}, bf16[128,4096]{1,0:T(8,128)(2,1)}, u32[]{:S(2)}) copy-start(bf16[128,4096]{1,0:T(8,128)(2,1)} %copy-done.6) | copy-start | bytes 3145732
  28.4 26.4 %collective-permute-start.4 = (bf16[512,256]{1,0:T(8,128)(2,1)S(1)}, bf16[512,256]{1,0:T(8,128)(2,1)S(1)}, u32[]{:S(2)}, u32[]{:S(2)}) collective-permute-start(bf16[512,256]{1,0:T(8,128)(2,1)S(1)} %get-tuple-element.40), channel_id=1, source_target_pairs={{0,128},{4,132},{8,136},{12,140},{16,144},{20,148},{24,152},{28,15... | collective-permute-start | bytes 786440 | tf_op jit(solution)/shard_map/ppermute | solution.py:328
  29.7 25.1 %collective-permute-start.3 = (bf16[512,256]{1,0:T(8,128)(2,1)S(1)}, bf16[512,256]{1,0:T(8,128)(2,1)S(1)}, u32[]{:S(2)}, u32[]{:S(2)}) collective-permute-start(bf16[512,256]{1,0:T(8,128)(2,1)S(1)} %get-tuple-element.39), channel_id=1, source_target_pairs={{0,128},{4,132},{8,136},{12,140},{16,144},{20,148},{24,152},{28,15... | collective-permute-start | bytes 786440 | tf_op jit(solution)/shard_map/ppermute | solution.py:328
  38.4 5.5 %copy-start.8 = (bf16[1,512,256]{2,1,0:T(8,128)(2,1)S(1)}, bf16[1,512,256]{2,1,0:T(8,128)(2,1)}, u32[]{:S(2)}) copy-start(bf16[1,512,256]{2,1,0:T(8,128)(2,1)} %param.11) | copy-start | bytes 786436
  38.4 14.9 %collective-permute-start.6 = (bf16[256,256]{1,0:T(8,128)(2,1)S(1)}, bf16[256,256]{1,0:T(8,128)(2,1)S(1)}, u32[]{:S(2)}, u32[]{:S(2)}) collective-permute-start(bf16[256,256]{1,0:T(8,128)(2,1)S(1)} %get-tuple-element.42), channel_id=1, source_target_pairs={{0,128},{4,132},{8,136},{12,140},{16,144},{20,148},{24,152},{28,15... | collective-permute-start | bytes 393224 | tf_op jit(solution)/shard_map/ppermute | solution.py:328
  43.8 10.9 %collective-permute-start.5 = (bf16[256,256]{1,0:T(8,128)(2,1)S(1)}, bf16[256,256]{1,0:T(8,128)(2,1)S(1)}, u32[]{:S(2)}, u32[]{:S(2)}) collective-permute-start(bf16[256,256]{1,0:T(8,128)(2,1)S(1)} %get-tuple-element.41), channel_id=1, source_target_pairs={{0,128},{4,132},{8,136},{12,140},{16,144},{20,148},{24,152},{28,15... | collective-permute-start | bytes 393224 | tf_op jit(solution)/shard_map/ppermute | solution.py:328
  43.9 10.8 %copy-start.9 = (s32[1,3]{1,0:T(1,128)S(1)}, s32[1,3]{1,0:T(1,128)}, u32[]{:S(2)}) copy-start(s32[1,3]{1,0:T(1,128)} %table_hbm.1) | copy-start | bytes 40

commit v4 on v3

--- a/solution.py
+++ b/solution.py
@@ -202,16 +202,17 @@
     depth_ref, q_ref, do_ref, qt_ref, dot_ref, l_ref, o_ref, kv_ref = refs[:8]
     split = block == 1
     from_ref = None if first else refs[8]
-    outs = refs[8 + (not first) + (split and start > 0) :]
+    outs = refs[8 + (not first) + split :]
+    other_ref = refs[9] if split and start == 0 else None
     dq_ref, g_ref = outs[:2]
-    next_ref = outs[2] if split and start == 0 else None
+    next_ref, both_ref = (outs[2], outs[3]) if split and start == 0 else (None, None)
     dk_ref, dv_ref = outs[-2:]
     many, dh = l_ref.shape
     step = many // 4
     size = g_ref.shape[0]
 
-    def work(keys, to):
-        k, v = kv_ref[start : start + keys, :dh], kv_ref[start : start + keys, dh:]
+    def work(keys, to, kv=kv_ref):
+        k, v = kv[start : start + keys, :dh], kv[start : start + keys, dh:]
         over = keys // dh
         for c in range(4):
             rs = slice(c * step, (c + 1) * step)
@@ -235,7 +236,16 @@
             ref[:, dh:] = dv_ref[:, ks].T.astype(BF16)
 
     if block == 0:
-        work(size, (g_ref,))
+
+        @pl.when(depth_ref[0] > 1)
+        def _():
+            work(size, (g_ref,))
+
+        @pl.when(depth_ref[0] <= 1)
+        def _():
+            dq_ref[...] = jnp.zeros_like(dq_ref)
+            g_ref[...] = jnp.zeros_like(g_ref)
+
         return
 
     @pl.when(depth_ref[0] == NSL - 1)
@@ -244,24 +254,30 @@
 
     if split and start > 0:
         return
-    unused = depth_ref[0] <= block
-    if split:
-
-        @pl.when(depth_ref[0] == NSL - 2)
+
+    @pl.when(depth_ref[0] < NSL - 1)
+    def _():
+        if not split:
+            g_ref[...] = jnp.zeros_like(g_ref)
+            return
+
+        @pl.when(depth_ref[0] > 1)
         def _():
-            work(2 * size, (g_ref, next_ref))
-
-    @pl.when(unused)
-    def _():
-        g_ref[...] = jnp.zeros_like(g_ref)
-        if split:
-            next_ref[...] = jnp.zeros_like(next_ref)
-
-
-def piece(depth, rows_of, kv, dq, held, block, start, size):
+            both_ref[...] = kv_ref[...]
+
+        @pl.when(depth_ref[0] <= 1)
+        def _():
+            both_ref[...] = other_ref[...]
+
+        work(2 * size, (g_ref, next_ref), both_ref)
+
+
+def piece(depth, rows_of, kv, other, dq, held, block, start, size):
     many, dh = rows_of[-1].shape
     split = block == 1
     args = (depth, *rows_of, kv) + (() if dq is None else (dq,)) + (() if held is None else (held,))
+    if split and start == 0:
+        args += (other,)
     gave = jax.ShapeDtypeStruct((size, 2 * dh), BF16)
     keys = 2 * size if split and start == 0 else size
     return pl.pallas_call(
@@ -269,7 +285,8 @@
         in_specs=[SMEM] + [VMEM] * (len(args) - 1),
         out_specs=[VMEM] * (3 if split and start == 0 else 2),
         out_shape=[jax.ShapeDtypeStruct((many, dh), F32), gave] + ([gave] if split and start == 0 else []),
-        scratch_shapes=[pltpu.VMEM((dh, keys), F32), pltpu.VMEM((dh, keys), F32)],
+        scratch_shapes=([pltpu.VMEM(kv.shape, BF16)] if split and start == 0 else [])
+        + [pltpu.VMEM((dh, keys), F32), pltpu.VMEM((dh, keys), F32)],
         input_output_aliases=({} if dq is None else {8: 0}) | ({} if held is None else {9: 1}),
         compiler_params=params(24),
         cost_estimate=cost(many, size, 1, dh),
@@ -277,11 +294,12 @@
     )(*args)
 
 
-def place_kernel(rows, table_ref, *refs):
+def place_kernel(rows, table_ref, depth_ref, *refs):
     ins, out_ref, sem = refs[: len(PIECES)], refs[-2], refs[-1]
     copies = []
     for i, (block, first, size) in enumerate(PIECES):
-        at = pl.multiple_of(table_ref[block] * rows + first, 128)
+        slot = table_ref[block] if block > 1 else table_ref[jnp.where(depth_ref[0] > 1, block, 1 - block)]
+        at = pl.multiple_of(slot * rows + first, 128)
         copies.append(pltpu.make_async_copy(ins[i], out_ref.at[pl.ds(at, size), :], sem.at[i]))
     for c in copies:
         c.start()
@@ -289,16 +307,16 @@
         c.wait()
 
 
-def place(table, parts, shape, rows):
+def place(table, depth, parts, shape, rows):
     return pl.pallas_call(
         functools.partial(place_kernel, rows),
-        in_specs=[SMEM] + [VMEM] * len(parts),
+        in_specs=[SMEM, SMEM] + [VMEM] * len(parts),
         out_specs=HBM,
         out_shape=jax.ShapeDtypeStruct(shape, BF16),
         scratch_shapes=[pltpu.SemaphoreType.DMA((len(PIECES),))],
         compiler_params=params(4),
         name="place",
-    )(table, *parts)
+    )(table, depth, *parts)
 
 
 def per_device(query, grad_output, log_total, offset, slice_keys, pool_keys, block_table):
@@ -310,6 +328,8 @@
     depths = [NSL - 1 - layer // group % (NSL - 1) for layer in range(sections)]
     me = lax.axis_index("section")
     depth = (NSL - 1 - me // group % (NSL - 1)).astype(jnp.int32).reshape(1)
+    partner = (me + half_axis) % sections
+    partner_depth = (NSL - 1 - partner // group % (NSL - 1)).astype(jnp.int32).reshape(1)
 
     swap = [(layer, (layer + half_axis) % sections) for layer in range(sections)]
     home = [(layer, p) for layer, p in swap if depths[layer] == NSL - 1]
@@ -323,11 +343,11 @@
     dq = held = None
     parts = []
     for block, start, size in PIECES:
-        dq, g, *rest = piece(depth, rows_of, arrived[block], dq, held, block, start, size)
+        dq, g, *rest = piece(depth, rows_of, arrived[block], arrived[0], dq, held, block, start, size)
         held = rest[0] if rest else None
         parts.append(lax.ppermute(g, "section", home if block == NSL - 2 else swap))
     query_grad, slice_grad = own(rows_of, slice_keys[0], dq)
-    pool_grad = place(table, parts, pool_keys.shape[1:], rows)
+    pool_grad = place(table, partner_depth, parts, pool_keys.shape[1:], rows)
     return (query_grad[None], slice_grad[None], pool_grad[None])
 
 

time: 56.8 us -> 56.8 us (level)
  waiting for transfers between devices: 6.3 us -> 2.38 us
  starting transfers between devices: 21.5 us -> 24.2 us
  Pallas kernels: 18.1 us -> 19.4 us
    ppermute x4, waiting for transfers between devices: 6.29 us -> 2.37 us  [per_device(): parts.append(lax.ppermute(g, 'section', home if block == NSL - 2 else swap))]
    ppermute x4, starting transfers between devices: 15.3 us -> 18 us  [per_device(): parts.append(lax.ppermute(g, 'section', home if block == NSL - 2 else swap))]
    pallas_call x4, Pallas kernels: 6.9 us -> 8.13 us  [piece(): pl.pallas_call(functools.partial(piece_kernel, many // kv.shape[0], dh **...]
  transfers between devices with their start and end apart: 7 -> 7, of which waited for: 2 -> 2; matrix products, arithmetic and copies ran while one was open for 0% -> 0% of each run, Pallas kernels for 25% -> 27%
where the time goes in v4:
time: 56.8 us; the launch traced here: 56.4 us
  starting transfers between devices  24.2 us (43%)
  Pallas kernels  19.4 us (34%)
  local copies, waits for them, and re-layouts  9.5 us (17%)
  waiting for transfers between devices  2.38 us (4%)
  between operations  0.91 us (2%)
    ppermute x4, starting transfers between devices, per_device(): parts.append(lax.ppermute(g, 'section', home if block == NSL - 2 else swap))  18 us
    unnamed x20, local copies, waits for them, and re-layouts  9.5 us
    pallas_call x4, Pallas kernels, piece(): pl.pallas_call(functools.partial(piece_kernel, many // kv.shape[0], dh **...  8.13 us
    ppermute x3, starting transfers between devices, per_device(): lax.ppermute(picked[i], 'section', deep if block == NSL - 2 else swap)  6.22 us
    pallas_call x1, Pallas kernels, own(): pl.pallas_call(functools.partial(own_kernel, heads, dh ** (-0.5)), in_spe...  4.49 us
    pallas_call x1, Pallas kernels, pick(): pl.pallas_call(functools.partial(pick_kernel, rows), in_specs=[HBM, HBM],...  2.69 us
    pallas_call x1, Pallas kernels, prep(): pl.pallas_call(functools.partial(prep_kernel, heads, dh), in_specs=[HBM]...  2.6 us
    ppermute x4, waiting for transfers between devices, per_device(): parts.append(lax.ppermute(g, 'section', home if block == NSL - 2 else swap))  2.37 us
  transfers between devices with their start and end apart: 7, of which 2 were waited for; matrix products, arithmetic and copies ran while one was open for 0% of the time, Pallas kernels for 27%

profile of v4, /device:TPU:28, one launch (start us, length us, event | category | flops | bytes accessed | tf_op | source)
XLA Modules:
  0.0 56.4 jit_solution(7896995056044629160)
XLA Ops:
  0.6 2.7 %pick.1 = (bf16[512,256]{1,0:T(8,128)(2,1)}, bf16[512,256]{1,0:T(8,128)(2,1)}, bf16[512,256]{1,0:T(8,128)(2,1)}) custom-call(s32[1,3]{1,0:T(1,128)} %table_hbm.1, bf16[1536,256]{1,0:T(8,128)(2,1)} %bitcast.20), custom_call_target="tpu_custom_call" | custom-call | tf_op jit(solution)/shard_map/pick/pallas_call | solution.py:57
  3.3 0.6 %collective-permute-start.2 = (bf16[512,256]{1,0:T(8,128)(2,1)}, bf16[512,256]{1,0:T(8,128)(2,1)}, u32[]{:S(2)}, u32[]{:S(2)}) collective-permute-start(bf16[512,256]{1,0:T(8,128)(2,1)} %get-tuple-element.31), channel_id=1, source_target_pairs={{0,128},{4,132},{8,136},{12,140},{16,144},{20,148},{24,152},{28,15... | collective-permute-start | bytes 786440 | tf_op jit(solution)/shard_map/ppermute | solution.py:341
  3.9 5.6 %collective-permute-start.1 = (bf16[512,256]{1,0:T(8,128)(2,1)}, bf16[512,256]{1,0:T(8,128)(2,1)}, u32[]{:S(2)}, u32[]{:S(2)}) collective-permute-start(bf16[512,256]{1,0:T(8,128)(2,1)} %get-tuple-element.30), channel_id=1, source_target_pairs={{128,0},{132,4},{136,8},{140,12},{144,16},{148,20},{152,24},{156,2... | collective-permute-start | bytes 786440 | tf_op jit(solution)/shard_map/ppermute | solution.py:341
  9.5 0.0 collective-permute-start
  9.6 2.6 %prep.1 = (bf16[512,1024]{1,0:T(8,128)(2,1)S(1)}, bf16[512,1024]{1,0:T(8,128)(2,1)S(1)}, bf16[128,4096]{1,0:T(8,128)(2,1)S(1)}, bf16[128,4096]{1,0:T(8,128)(2,1)...) custom-call(bf16[512,1024]{1,0:T(8,128)(2,1)} %bitcast.18, bf16[512,1024]{1,0:T(8,128)(2,1)} %bitcast.19, ...), custom_call_target="tpu_custom_call" | custom-call | flops 1000 | bytes 4194304 | tf_op jit(solution)/shard_map/prep/pallas_call | solution.py:110
  12.2 0.0 copy-start
  12.2 1.3 %copy-done = f32[4096,128]{1,0:T(8,128)} copy-done((f32[4096,128]{1,0:T(8,128)}, f32[4096,128]{1,0:T(8,128)S(1)}, u32[]{:S(2)}) %copy-start) | copy-done | bytes 2097176
  13.5 0.0 copy-start.2
  13.5 1.0 %copy-done.2 = bf16[512,1024]{1,0:T(8,128)(2,1)} copy-done((bf16[512,1024]{1,0:T(8,128)(2,1)}, bf16[512,1024]{1,0:T(8,128)(2,1)S(1)}, u32[]{:S(2)}) %copy-start.2) | copy-done | bytes 1048600
  14.5 0.0 copy-start.4
  14.5 1.0 %copy-done.4 = bf16[128,4096]{1,0:T(8,128)(2,1)} copy-done((bf16[128,4096]{1,0:T(8,128)(2,1)}, bf16[128,4096]{1,0:T(8,128)(2,1)S(1)}, u32[]{:S(2)}) %copy-start.4) | copy-done | bytes 1048600
  15.4 0.0 copy-start.6
  15.4 1.0 %copy-done.6 = bf16[128,4096]{1,0:T(8,128)(2,1)} copy-done((bf16[128,4096]{1,0:T(8,128)(2,1)}, bf16[128,4096]{1,0:T(8,128)(2,1)S(1)}, u32[]{:S(2)}) %copy-start.6) | copy-done | bytes 1048600
  16.4 0.0 collective-permute-done.2.refs_7_.refs_9_
  16.4 0.0 copy-start.1
  16.4 1.6 %copy-done.1 = f32[4096,128]{1,0:T(8,128)S(1)} copy-done((f32[4096,128]{1,0:T(8,128)S(1)}, f32[4096,128]{1,0:T(8,128)}, u32[]{:S(2)}) %copy-start.1) | copy-done | bytes 2097176
  18.0 0.0 copy-start.3
  18.0 1.2 %copy-done.3 = bf16[512,1024]{1,0:T(8,128)(2,1)S(1)} copy-done((bf16[512,1024]{1,0:T(8,128)(2,1)S(1)}, bf16[512,1024]{1,0:T(8,128)(2,1)}, u32[]{:S(2)}) %copy-start.3) | copy-done | bytes 1048600
  19.2 0.0 copy-start.5
  19.2 1.2 %copy-done.5 = bf16[128,4096]{1,0:T(8,128)(2,1)S(1)} copy-done((bf16[128,4096]{1,0:T(8,128)(2,1)S(1)}, bf16[128,4096]{1,0:T(8,128)(2,1)}, u32[]{:S(2)}) %copy-start.5) | copy-done | bytes 1048600
  20.4 0.0 copy-start.7
  20.4 1.2 %copy-done.7 = bf16[128,4096]{1,0:T(8,128)(2,1)S(1)} copy-done((bf16[128,4096]{1,0:T(8,128)(2,1)S(1)}, bf16[128,4096]{1,0:T(8,128)(2,1)}, u32[]{:S(2)}) %copy-start.7) | copy-done | bytes 1048600
  21.7 1.1 %piece.4 = (f32[4096,128]{1,0:T(8,128)S(1)}, bf16[512,256]{1,0:T(8,128)(2,1)S(1)}) custom-call(s32[1]{0:T(128)} %bitcast.7.refs_0_, bf16[512,1024]{1,0:T(8,128)(2,1)S(1)} %get-tuple-element.23.refs_1_.q_ref, bf16[512,1024]{1,0:T(8,128)(2,1)S(1)} %copy-done.3, bf16[128,4096]{1,0:T(8,128)(2,1)S(1)} %copy-done.5, bf16[128,4096]{1,0:T(8,128)(2,1)S(1)} %copy-done.7, ...), custom_call_target="tpu_custom_call" | custom-call | flops 2684354560 | bytes 1048576 | tf_op jit(solution)/shard_map/piece/pallas_call | solution.py:283
  22.8 0.0 collective-permute-done.1.refs_7_
  22.8 1.0 %piece.5 = (f32[4096,128]{1,0:T(8,128)S(1)}, bf16[512,256]{1,0:T(8,128)(2,1)S(1)}) custom-call(s32[1]{0:T(128)} %bitcast.7.refs_0_, bf16[512,1024]{1,0:T(8,128)(2,1)S(1)} %get-tuple-element.23.refs_1_.q_ref, bf16[512,1024]{1,0:T(8,128)(2,1)S(1)} %copy-done.3, bf16[128,4096]{1,0:T(8,128)(2,1)S(1)} %copy-done.5, ...), custom_call_target="tpu_custom_call", output_to_operand_aliasing={{0}: (8, {})} | custom-call | flops 2684354560 | bytes 1048576 | tf_op jit(solution)/shard_map/piece/pallas_call | solution.py:283
  23.8 1.3 %collective-permute-start.4 = (bf16[512,256]{1,0:T(8,128)(2,1)S(1)}, bf16[512,256]{1,0:T(8,128)(2,1)S(1)}, u32[]{:S(2)}, u32[]{:S(2)}) collective-permute-start(bf16[512,256]{1,0:T(8,128)(2,1)S(1)} %get-tuple-element.40), channel_id=1, source_target_pairs={{0,128},{4,132},{8,136},{12,140},{16,144},{20,148},{24,152},{28,15... | collective-permute-start | bytes 786440 | tf_op jit(solution)/shard_map/ppermute | solution.py:348
  25.1 13.1 %collective-permute-start.3 = (bf16[512,256]{1,0:T(8,128)(2,1)S(1)}, bf16[512,256]{1,0:T(8,128)(2,1)S(1)}, u32[]{:S(2)}, u32[]{:S(2)}) collective-permute-start(bf16[512,256]{1,0:T(8,128)(2,1)S(1)} %get-tuple-element.39), channel_id=1, source_target_pairs={{0,128},{4,132},{8,136},{12,140},{16,144},{20,148},{24,152},{28,15... | collective-permute-start | bytes 786440 | tf_op jit(solution)/shard_map/ppermute | solution.py:348
  38.1 0.0 collective-permute-done.refs_7_
  38.1 6.0 %piece.6 = (f32[4096,128]{1,0:T(8,128)S(1)}, bf16[256,256]{1,0:T(8,128)(2,1)S(1)}, bf16[256,256]{1,0:T(8,128)(2,1)S(1)}) custom-call(s32[1]{0:T(128)} %bitcast.7.refs_0_, bf16[512,1024]{1,0:T(8,128)(2,1)S(1)} %get-tuple-element.23.refs_1_.q_ref, bf16[512,1024]{1,0:T(8,128)(2,1)S(1)} %copy-done.3, ...), custom_call_target="tpu_custom_call", output_to_operand_aliasing={{0}: (8, {})} | custom-call | flops 1342177280 | bytes 1048576 | tf_op jit(solution)/shard_map/piece/pallas_call | solution.py:283
  44.2 0.0 copy-start.8
  44.2 0.5 collective-permute-start.6
  44.8 3.1 %collective-permute-start.5 = (bf16[256,256]{1,0:T(8,128)(2,1)S(1)}, bf16[256,256]{1,0:T(8,128)(2,1)S(1)}, u32[]{:S(2)}, u32[]{:S(2)}) collective-permute-start(bf16[256,256]{1,0:T(8,128)(2,1)S(1)} %get-tuple-element.41), channel_id=1, source_target_pairs={{0,128},{4,132},{8,136},{12,140},{16,144},{20,148},{24,152},{28,15... | collective-permute-start | bytes 393224 | tf_op jit(solution)/shard_map/ppermute | solution.py:348
  47.8 0.0 copy-done.8
  47.8 0.0 copy-start.9
  47.9 4.5 %own.1 = (bf16[512,1024]{1,0:T(8,128)(2,1)}, bf16[512,256]{1,0:T(8,128)(2,1)}) custom-call(bf16[512,1024]{1,0:T(8,128)(2,1)S(1)} %get-tuple-element.23.refs_1_.q_ref, bf16[512,1024]{1,0:T(8,128)(2,1)S(1)} %copy-done.3, bf16[128,4096]{1,0:T(8,128)(2,1)S(1)} %copy-done.5, bf16[128,4096]{1,0:T(8,128)(2,1)S(1)} %copy-done.7, ...), custom_call_target="tpu_custom_call" | custom-call | flops 2013265920 | bytes 1048576 | tf_op jit(solution)/shard_map/own/pallas_call | solution.py:183
  52.3 1.0 %collective-permute-done.6.refs_3_ = bf16[256,256]{1,0:T(8,128)(2,1)S(1)} collective-permute-done((bf16[256,256]{1,0:T(8,128)(2,1)S(1)}, bf16[256,256]{1,0:T(8,128)(2,1)S(1)}, u32[]{:S(2)}, u32[]{:S(2)}) %collective-permute-start.6) | collective-permute-done | bytes 131104 | tf_op jit(solution)/shard_map/ppermute | solution.py:348
  53.3 1.4 %collective-permute-done.5.refs_2_ = bf16[256,256]{1,0:T(8,128)(2,1)S(1)} collective-permute-done((bf16[256,256]{1,0:T(8,128)(2,1)S(1)}, bf16[256,256]{1,0:T(8,128)(2,1)S(1)}, u32[]{:S(2)}, u32[]{:S(2)}) %collective-permute-start.5) | collective-permute-done | bytes 131104 | tf_op jit(solution)/shard_map/ppermute | solution.py:348
  54.7 0.0 collective-permute-done.4.refs_1_
  54.7 0.0 collective-permute-done.3.refs_0_
  54.7 0.0 copy-done.9
  54.7 1.5 %place.1 = bf16[1536,256]{1,0:T(8,128)(2,1)} custom-call(s32[3]{0:T(128)S(1)} %bitcast.17, s32[1]{0:T(128)} %bitcast.12.depth_ref, bf16[512,256]{1,0:T(8,128)(2,1)S(1)} %collective-permute-done.3.refs_0_, bf16[512,256]{1,0:T(8,128)(2,1)S(1)} %collective-permute-done.4.refs_1_, bf16[256,256]{1,0:T(8,128)(2,1)S(1)} %collective-permute-done.5.refs_2_, ...), custom_call_target="tpu_custom_call" | custom-call | tf_op jit(solution)/shard_map/place/pallas_call | solution.py:311
  (1 shorter events, 0.0 us)
Async XLA Ops:
  3.3 13.1 %collective-permute-start.2 = (bf16[512,256]{1,0:T(8,128)(2,1)}, bf16[512,256]{1,0:T(8,128)(2,1)}, u32[]{:S(2)}, u32[]{:S(2)}) collective-permute-start(bf16[512,256]{1,0:T(8,128)(2,1)} %get-tuple-element.31), channel_id=1, source_target_pairs={{0,128},{4,132},{8,136},{12,140},{16,144},{20,148},{24,152},{28,15... | collective-permute-start | bytes 786440 | tf_op jit(solution)/shard_map/ppermute | solution.py:341
  3.9 18.9 %collective-permute-start.1 = (bf16[512,256]{1,0:T(8,128)(2,1)}, bf16[512,256]{1,0:T(8,128)(2,1)}, u32[]{:S(2)}, u32[]{:S(2)}) collective-permute-start(bf16[512,256]{1,0:T(8,128)(2,1)} %get-tuple-element.30), channel_id=1, source_target_pairs={{128,0},{132,4},{136,8},{140,12},{144,16},{148,20},{152,24},{156,2... | collective-permute-start | bytes 786440 | tf_op jit(solution)/shard_map/ppermute | solution.py:341
  9.5 28.6 %collective-permute-start = (bf16[512,256]{1,0:T(8,128)(2,1)}, bf16[512,256]{1,0:T(8,128)(2,1)S(1)}, u32[]{:S(2)}, u32[]{:S(2)}) collective-permute-start(bf16[512,256]{1,0:T(8,128)(2,1)} %get-tuple-element.29), channel_id=1, source_target_pairs={{0,128},{4,132},{8,136},{12,140},{16,144},{20,148},{24,152},{28,15... | collective-permute-start | bytes 786440 | tf_op jit(solution)/shard_map/ppermute | solution.py:341
  12.2 1.3 %copy-start = (f32[4096,128]{1,0:T(8,128)}, f32[4096,128]{1,0:T(8,128)S(1)}, u32[]{:S(2)}) copy-start(f32[4096,128]{1,0:T(8,128)S(1)} %get-tuple-element.28.refs_6_.o_ref) | copy-start | bytes 6291460
  13.5 1.0 %copy-start.2 = (bf16[512,1024]{1,0:T(8,128)(2,1)}, bf16[512,1024]{1,0:T(8,128)(2,1)S(1)}, u32[]{:S(2)}) copy-start(bf16[512,1024]{1,0:T(8,128)(2,1)S(1)} %get-tuple-element.24.refs_2_.do_ref) | copy-start | bytes 3145732
  14.5 1.0 %copy-start.4 = (bf16[128,4096]{1,0:T(8,128)(2,1)}, bf16[128,4096]{1,0:T(8,128)(2,1)S(1)}, u32[]{:S(2)}) copy-start(bf16[128,4096]{1,0:T(8,128)(2,1)S(1)} %get-tuple-element.25.refs_3_.qt_ref) | copy-start | bytes 3145732
  15.4 1.0 %copy-start.6 = (bf16[128,4096]{1,0:T(8,128)(2,1)}, bf16[128,4096]{1,0:T(8,128)(2,1)S(1)}, u32[]{:S(2)}) copy-start(bf16[128,4096]{1,0:T(8,128)(2,1)S(1)} %get-tuple-element.26.refs_4_.dot_ref) | copy-start | bytes 3145732
  16.4 1.6 %copy-start.1 = (f32[4096,128]{1,0:T(8,128)S(1)}, f32[4096,128]{1,0:T(8,128)}, u32[]{:S(2)}) copy-start(f32[4096,128]{1,0:T(8,128)} %copy-done) | copy-start | bytes 6291460
  18.0 1.2 %copy-start.3 = (bf16[512,1024]{1,0:T(8,128)(2,1)S(1)}, bf16[512,1024]{1,0:T(8,128)(2,1)}, u32[]{:S(2)}) copy-start(bf16[512,1024]{1,0:T(8,128)(2,1)} %copy-done.2) | copy-start | bytes 3145732
  19.2 1.2 %copy-start.5 = (bf16[128,4096]{1,0:T(8,128)(2,1)S(1)}, bf16[128,4096]{1,0:T(8,128)(2,1)}, u32[]{:S(2)}) copy-start(bf16[128,4096]{1,0:T(8,128)(2,1)} %copy-done.4) | copy-start | bytes 3145732
  20.4 1.2 %copy-start.7 = (bf16[128,4096]{1,0:T(8,128)(2,1)S(1)}, bf16[128,4096]{1,0:T(8,128)(2,1)}, u32[]{:S(2)}) copy-start(bf16[128,4096]{1,0:T(8,128)(2,1)} %copy-done.6) | copy-start | bytes 3145732
  23.8 31.0 %collective-permute-start.4 = (bf16[512,256]{1,0:T(8,128)(2,1)S(1)}, bf16[512,256]{1,0:T(8,128)(2,1)S(1)}, u32[]{:S(2)}, u32[]{:S(2)}) collective-permute-start(bf16[512,256]{1,0:T(8,128)(2,1)S(1)} %get-tuple-element.40), channel_id=1, source_target_pairs={{0,128},{4,132},{8,136},{12,140},{16,144},{20,148},{24,152},{28,15... | collective-permute-start | bytes 786440 | tf_op jit(solution)/shard_map/ppermute | solution.py:348
  25.1 29.7 %collective-permute-start.3 = (bf16[512,256]{1,0:T(8,128)(2,1)S(1)}, bf16[512,256]{1,0:T(8,128)(2,1)S(1)}, u32[]{:S(2)}, u32[]{:S(2)}) collective-permute-start(bf16[512,256]{1,0:T(8,128)(2,1)S(1)} %get-tuple-element.39), channel_id=1, source_target_pairs={{0,128},{4,132},{8,136},{12,140},{16,144},{20,148},{24,152},{28,15... | collective-permute-start | bytes 786440 | tf_op jit(solution)/shard_map/ppermute | solution.py:348
  44.2 3.7 %copy-start.8 = (bf16[1,512,256]{2,1,0:T(8,128)(2,1)S(1)}, bf16[1,512,256]{2,1,0:T(8,128)(2,1)}, u32[]{:S(2)}) copy-start(bf16[1,512,256]{2,1,0:T(8,128)(2,1)} %param.11) | copy-start | bytes 786436
  44.2 9.1 %collective-permute-start.6 = (bf16[256,256]{1,0:T(8,128)(2,1)S(1)}, bf16[256,256]{1,0:T(8,128)(2,1)S(1)}, u32[]{:S(2)}, u32[]{:S(2)}) collective-permute-start(bf16[256,256]{1,0:T(8,128)(2,1)S(1)} %get-tuple-element.42), channel_id=1, source_target_pairs={{0,128},{4,132},{8,136},{12,140},{16,144},{20,148},{24,152},{28,15... | collective-permute-start | bytes 393224 | tf_op jit(solution)/shard_map/ppermute | solution.py:348
  44.8 9.9 %collective-permute-start.5 = (bf16[256,256]{1,0:T(8,128)(2,1)S(1)}, bf16[256,256]{1,0:T(8,128)(2,1)S(1)}, u32[]{:S(2)}, u32[]{:S(2)}) collective-permute-start(bf16[256,256]{1,0:T(8,128)(2,1)S(1)} %get-tuple-element.41), channel_id=1, source_target_pairs={{0,128},{4,132},{8,136},{12,140},{16,144},{20,148},{24,152},{28,15... | collective-permute-start | bytes 393224 | tf_op jit(solution)/shard_map/ppermute | solution.py:348
  47.8 6.9 %copy-start.9 = (s32[1,3]{1,0:T(1,128)S(1)}, s32[1,3]{1,0:T(1,128)}, u32[]{:S(2)}) copy-start(s32[1,3]{1,0:T(1,128)} %table_hbm.1) | copy-start | bytes 40
